TPU v7x, 32 devices: a whole 2x2x4 slice. The times are simulated.
32 devices in a mesh: grp: 2 (over y), ctx: 4 (over z), chan: 4 (over x, core).
Axes of the slice: x: 2, y: 2, z: 4, core: 2. Of those that a mesh axis runs over, the one named last changes fastest.
Arguments:
- grad_out: bfloat16 [1024, 4096], P(('grp', 'ctx'), 'chan'), parts along dimension 0, may hold values from -6 to 6
- gate_act: bfloat16 [1024, 4096], P(('grp', 'ctx'), 'chan'), parts along dimension 0, may hold values from -6 to 6
- conv_input: bfloat16 [1024, 4096], P(('grp', 'ctx'), 'chan'), parts along dimension 0, may hold values from -0.26367188 to 0.26367188
- filter_taps: bfloat16 [512, 4096], P('ctx', 'chan'), may hold values from -0.26367188 to 0.26367188
- skip_gain: float32 [4096], P('chan'), may hold values from -4 to 4
Outputs:
- grad_input: bfloat16 [1024, 4096], P(('grp', 'ctx'), 'chan'), parts along dimension 0
- grad_filter: float32 [1024, 4096], P(('grp', 'ctx'), 'chan'), parts along dimension 0
There are 2 independent parts, one for each index of `grp`. A program takes and returns all parts, laid end to end along the dimension named above; an argument that names none is the same for every part. Nothing has to cross between parts.
All inputs are finite; a program needn't handle non-finite values.
Results may differ from a plain program's by a relative error of at most 0.014.
Values may be sent and summed in bfloat16 or wider, within the bound.
No kernel may reach another device: no remote copies, remote signals or barrier semaphores. Data moves between devices by JAX's collectives and lax.ppermute only.
A program may use at most 64 MiB of HBM per device.

v0:
```python
import jax
import jax.numpy as jnp
from jax import lax
from jax.sharding import PartitionSpec as P


def split_parts(values):
    high_part = values.astype(jnp.bfloat16)
    low_part = (values - high_part.astype(jnp.float32)).astype(jnp.bfloat16)
    return (high_part, low_part)


def phase_tables(row_count, col_count, shift, period):
    row_index = jnp.arange(row_count, dtype=jnp.int32)[:, None] + shift
    col_index = jnp.arange(col_count, dtype=jnp.int32)[None, :]
    angles = (row_index * col_index % period).astype(jnp.float32) * (2.0 * jnp.pi / period)
    return (split_parts(jnp.cos(angles)), split_parts(jnp.sin(angles)))


def table_times(table, signal):
    high_part, low_part = table
    return jnp.dot(high_part, signal, preferred_element_type=jnp.float32) + jnp.dot(
        low_part, signal, preferred_element_type=jnp.float32
    )


def table_times_float(table, values):
    high_part, low_part = table
    value_high, value_low = split_parts(values)
    total = jnp.dot(high_part, value_high, preferred_element_type=jnp.float32)
    total = total + jnp.dot(high_part, value_low, preferred_element_type=jnp.float32)
    return total + jnp.dot(low_part, value_high, preferred_element_type=jnp.float32)


def forward_spectra(tables, signal):
    cos_part, sin_part = tables
    return (table_times(cos_part, signal), -table_times(sin_part, signal))


def inverse_spectra(tables, spectra, period):
    cos_part, sin_part = tables
    return (
        table_times_float(cos_part, spectra[0]) - table_times_float(sin_part, spectra[1])
    ) / period


def batched_times(table, blocks):
    high_part, low_part = table
    return jnp.einsum(
        "pr,nrc->npc", high_part, blocks, preferred_element_type=jnp.float32
    ) + jnp.einsum("pr,nrc->npc", low_part, blocks, preferred_element_type=jnp.float32)


def times_conj(first_spec, second_spec):
    return (
        first_spec[0] * second_spec[0] + first_spec[1] * second_spec[1],
        first_spec[1] * second_spec[0] - first_spec[0] * second_spec[1],
    )


def shards(grad_out, gate_act, conv_input, filter_taps, skip_gain):
    span_len = grad_out.shape[0]
    channels = grad_out.shape[1]
    period = 2 * span_len
    cycle_size = lax.axis_size("ctx")
    own_index = lax.axis_index("ctx")
    grad_y = (grad_out.astype(jnp.float32) * gate_act.astype(jnp.float32)).astype(jnp.bfloat16)
    short_fwd = phase_tables(period, span_len, 0, period)
    full_fwd = phase_tables(period, period, 0, period)
    short_inv = phase_tables(span_len, period, span_len, period)
    full_inv = phase_tables(period, period, span_len, period)
    taps = lax.all_gather(filter_taps, "ctx", axis=0, tiled=True)
    taps_padded = jnp.concatenate([jnp.zeros((span_len, channels), jnp.bfloat16), taps], axis=0)
    windows = jnp.concatenate(
        [
            taps_padded[:-span_len].reshape(cycle_size, span_len, channels),
            taps_padded[span_len:].reshape(cycle_size, span_len, channels),
        ],
        axis=1,
    )
    window_real = batched_times(full_fwd[0], windows)
    window_imag = -batched_times(full_fwd[1], windows)
    own_input_spec = forward_spectra(short_fwd, conv_input)
    zero_spec = jnp.zeros((period, channels), jnp.float32)
    lag_sums = jnp.zeros((taps_padded.shape[0], channels), jnp.float32)

    def add_pair(lag_totals, grad_spec, input_spec, distance):
        window_spec = (
            lax.dynamic_index_in_dim(window_real, distance, 0, keepdims=False),
            lax.dynamic_index_in_dim(window_imag, distance, 0, keepdims=False),
        )
        product = times_conj(grad_spec, window_spec)
        start_row = distance * span_len
        lag_window = inverse_spectra(full_inv, times_conj(grad_spec, input_spec), period)
        current = lax.dynamic_slice_in_dim(lag_totals, start_row, period, 0)
        lag_totals = lax.dynamic_update_slice_in_dim(lag_totals, current + lag_window, start_row, 0)
        return (product, lag_totals)

    spans = lax.all_gather(grad_y[None], "ctx", axis=0, tiled=True)

    def span_step(offset, current):
        distance = offset - own_index

        def run_pair(values_now):
            arrived = lax.dynamic_index_in_dim(spans, offset, 0, keepdims=False)
            product, new_sums = add_pair(
                values_now[2], forward_spectra(short_fwd, arrived), own_input_spec, distance
            )
            return (values_now[0] + product[0], values_now[1] + product[1], new_sums)

        return lax.cond(distance >= 0, run_pair, lambda values_now: values_now, current)

    home_real, home_imag, lag_sums = lax.fori_loop(
        0, spans.shape[0], span_step, (zero_spec, zero_spec, lag_sums)
    )
    conv_part = inverse_spectra(short_inv, (home_real, home_imag), period)
    grad_input = (conv_part + skip_gain[None, :] * grad_y.astype(jnp.float32)).astype(jnp.bfloat16)
    grad_filter = lax.psum_scatter(
        lag_sums[span_len:].astype(jnp.bfloat16), "ctx", scatter_dimension=0, tiled=True
    ).astype(jnp.float32)
    return (grad_input, grad_filter)


def solution(mesh):
    return jax.shard_map(
        shards,
        mesh=mesh,
        in_specs=(
            P(("grp", "ctx"), "chan"),
            P(("grp", "ctx"), "chan"),
            P(("grp", "ctx"), "chan"),
            P("ctx", "chan"),
            P("chan"),
        ),
        out_specs=(P(("grp", "ctx"), "chan"), P(("grp", "ctx"), "chan")),
        check_vma=False,
    )
```

profile of v0, /device:TPU:0, one launch (start us, length us, event | category | flops | bytes accessed | tf_op | source)
XLA Modules:
  0.0 181.5 jit_solution(1788791915903343266)
XLA Ops:
  8.0 1.8 multiply_convert_fusion
  15.4 24.8 %all-gather.4.cloned.1.call-done = bf16[512,1024]{1,0:T(8,128)(2,1)} async-done(((bf16[128,1024]{1,0:T(8,128)(2,1)}), bf16[512,1024]{1,0:T(8,128)(2,1)}) %all-gather.4.cloned.1.call-update) | async-done | bytes 1048592 | tf_op jit(solution)/shard_map/all_gather | solution.py:72
  46.4 3.6 %add_bitcast_fusion = f32[4,256,1024]{1,2,0:T(8,128)} fusion(f32[4,1024,256]{2,1,0:T(8,128)S(1)} %fusion.93, bf16[4,128,1024]{1,2,0:T(8,128)(2,1)S(1)} %copy.11, bf16[4,128,1024]{1,2,0:T(8,128)(2,1)S(1)} %copy.10), kind=kOutput, calls=%fused_computation.87 | convolution fusion | flops 543293440 | bytes 10485760 | tf_op jit(solution)/shard_map/pr,nrc->npc/dot_general | solution.py:51
  50.0 3.7 %negate_bitcast_fusion = f32[4,256,1024]{1,2,0:T(8,128)} fusion(f32[4,1024,256]{2,1,0:T(8,128)S(1)} %fusion.91, bf16[4,128,1024]{1,2,0:T(8,128)(2,1)S(1)} %copy.11, bf16[4,128,1024]{1,2,0:T(8,128)(2,1)S(1)} %copy.10), kind=kOutput, calls=%fused_computation.86 | convolution fusion | flops 544342016 | bytes 10485760 | tf_op jit(solution)/shard_map/pr,nrc->npc/dot_general | solution.py:51
  53.7 16.3 %all-gather.6.cloned.1.call-done = bf16[512,1024]{1,0:T(8,128)(2,1)} async-done(((bf16[128,1024]{1,0:T(8,128)(2,1)}), bf16[512,1024]{1,0:T(8,128)(2,1)}) %all-gather.6.cloned.1.call-update) | async-done | bytes 1048592 | tf_op jit(solution)/shard_map/all_gather | solution.py:99
  70.0 1.7 broadcast_in_dim.7
  73.9 70.8 %while.20 = (s32[]{:T(128)}, f32[256,1024]{0,1:T(8,128)}, f32[256,1024]{0,1:T(8,128)}, f32[640,1024]{0,1:T(8,128)}, s32[]{:T(128)}, /*index=5*/bf16[4,128,1024]{...) while((s32[]{:T(128)}, f32[256,1024]{0,1:T(8,128)}, ...), condition=%wide.region_3.4_spmd.clone.clone.clone, body=%wide.region_0.3_spmd.clone.clone.clone.sunk | while | flops 1085865984 | bytes 40109640 | solution.py:113
  73.9 1.9 %subtract_convert_fusion.25 = (bf16[256,256]{1,0:T(8,128)(2,1)}, bf16[256,256]{1,0:T(8,128)(2,1)}, bf16[256,256]{1,0:T(8,128)(2,1)S(1)}, bf16[256,256]{1,0:T(8,128)(2,1)}) fusion(s32[256]{0:T(256)S(1)} %get-tuple-element.688), kind=kLoop, calls=%fused_computation.62.clone.1 | loop fusion | flops 1441792 | bytes 525312 | tf_op jit(solution)/shard_map/convert_element_type | solution.py:9
  78.1 13.5 %conditional.5 = ((f32[256,1024]{0,1:T(8,128)}, f32[256,1024]{0,1:T(8,128)}, f32[640,1024]{0,1:T(8,128)})) conditional(s32[]{:T(128)} %convert_element_type.670, (f32[256,1024]{0,1:T(8,128)}, f32[256,1024]{0,1:T(8,128)}, f32[640,1024]{0,1:T(8,128)}) %tuple.73, (s32[]{:T(128)}, bf16[4,128,1024]{2,1,0:T(8,128)(2,1)}, bf16[256,128]{1,0:T(8,128)(2,1)}, ...), branch_computations={%region_1.1_spmd, %region_2.2_spmd} | conditional | flops 1083179008 | bytes 39321852 | solution.py:111
  82.0 5.0 %multiply_subtract_fusion = (f32[256,1024]{0,1:T(8,128)S(1)}, f32[256,1024]{0,1:T(8,128)S(1)}, f32[256,1024]{0,1:T(8,128)}, f32[256,1024]{0,1:T(8,128)}) fusion(f32[256,1024]{0,1:T(8,128)} %get-tuple-element.336, f32[256,1024]{0,1:T(8,128)S(1)} %fusion.22, f32[256,1024]{0,1:T(8,128)} %get-tuple-element.335, f32[256,1024]{0,1:T(8,128)} %get-tuple-element.323, ...), kind=kOutput, calls=%fused_computation.31 | convolution fusion | flops 71041024 | bytes 12910600 | tf_op jit(solution)/shard_map/while/body/eval_jaxpr/cond/branch_1_fun/dot_general | solution.py:22
  88.9 2.7 %fusion.20 = f32[640,1024]{0,1:T(8,128)} fusion(f32[640,1024]{0,1:T(8,128)} %get-tuple-element.334, s32[]{:T(128)S(6)} %select_n.24, f32[1024,256]{1,0:T(8,128)S(1)} %convolution_add_fusion.2, f32[1024,256]{1,0:T(8,128)S(1)} %convolution_add_fusion.1, bf16[256,256]{1,0:T(8,128)(2,1)S(1)} %copy-done.2, f32[256,1024]{0,1:T(8,128)S(1)} %get-tuple-element.545), kind=kOutput, calls=%fused_computation.13 | convolution fusion | flops 135528448 | bytes 5373956 | tf_op jit(solution)/shard_map/while/body/eval_jaxpr/cond/branch_1_fun/dot_general | solution.py:32
  91.6 1.9 %subtract_convert_fusion.25 = (bf16[256,256]{1,0:T(8,128)(2,1)}, bf16[256,256]{1,0:T(8,128)(2,1)}, bf16[256,256]{1,0:T(8,128)(2,1)S(1)}, bf16[256,256]{1,0:T(8,128)(2,1)}) fusion(s32[256]{0:T(256)S(1)} %get-tuple-element.688), kind=kLoop, calls=%fused_computation.62.clone.1 | loop fusion | flops 1441792 | bytes 525312 | tf_op jit(solution)/shard_map/convert_element_type | solution.py:9
  95.9 13.5 %conditional.5 = ((f32[256,1024]{0,1:T(8,128)}, f32[256,1024]{0,1:T(8,128)}, f32[640,1024]{0,1:T(8,128)})) conditional(s32[]{:T(128)} %convert_element_type.670, (f32[256,1024]{0,1:T(8,128)}, f32[256,1024]{0,1:T(8,128)}, f32[640,1024]{0,1:T(8,128)}) %tuple.73, (s32[]{:T(128)}, bf16[4,128,1024]{2,1,0:T(8,128)(2,1)}, bf16[256,128]{1,0:T(8,128)(2,1)}, ...), branch_computations={%region_1.1_spmd, %region_2.2_spmd} | conditional | flops 1083179008 | bytes 39321852 | solution.py:111
  99.7 5.0 %multiply_subtract_fusion = (f32[256,1024]{0,1:T(8,128)S(1)}, f32[256,1024]{0,1:T(8,128)S(1)}, f32[256,1024]{0,1:T(8,128)}, f32[256,1024]{0,1:T(8,128)}) fusion(f32[256,1024]{0,1:T(8,128)} %get-tuple-element.336, f32[256,1024]{0,1:T(8,128)S(1)} %fusion.22, f32[256,1024]{0,1:T(8,128)} %get-tuple-element.335, f32[256,1024]{0,1:T(8,128)} %get-tuple-element.323, ...), kind=kOutput, calls=%fused_computation.31 | convolution fusion | flops 71041024 | bytes 12910600 | tf_op jit(solution)/shard_map/while/body/eval_jaxpr/cond/branch_1_fun/dot_general | solution.py:22
  106.6 2.7 %fusion.20 = f32[640,1024]{0,1:T(8,128)} fusion(f32[640,1024]{0,1:T(8,128)} %get-tuple-element.334, s32[]{:T(128)S(6)} %select_n.24, f32[1024,256]{1,0:T(8,128)S(1)} %convolution_add_fusion.2, f32[1024,256]{1,0:T(8,128)S(1)} %convolution_add_fusion.1, bf16[256,256]{1,0:T(8,128)(2,1)S(1)} %copy-done.2, f32[256,1024]{0,1:T(8,128)S(1)} %get-tuple-element.545), kind=kOutput, calls=%fused_computation.13 | convolution fusion | flops 135528448 | bytes 5373956 | tf_op jit(solution)/shard_map/while/body/eval_jaxpr/cond/branch_1_fun/dot_general | solution.py:32
  109.3 1.9 %subtract_convert_fusion.25 = (bf16[256,256]{1,0:T(8,128)(2,1)}, bf16[256,256]{1,0:T(8,128)(2,1)}, bf16[256,256]{1,0:T(8,128)(2,1)S(1)}, bf16[256,256]{1,0:T(8,128)(2,1)}) fusion(s32[256]{0:T(256)S(1)} %get-tuple-element.688), kind=kLoop, calls=%fused_computation.62.clone.1 | loop fusion | flops 1441792 | bytes 525312 | tf_op jit(solution)/shard_map/convert_element_type | solution.py:9
  113.6 13.4 %conditional.5 = ((f32[256,1024]{0,1:T(8,128)}, f32[256,1024]{0,1:T(8,128)}, f32[640,1024]{0,1:T(8,128)})) conditional(s32[]{:T(128)} %convert_element_type.670, (f32[256,1024]{0,1:T(8,128)}, f32[256,1024]{0,1:T(8,128)}, f32[640,1024]{0,1:T(8,128)}) %tuple.73, (s32[]{:T(128)}, bf16[4,128,1024]{2,1,0:T(8,128)(2,1)}, bf16[256,128]{1,0:T(8,128)(2,1)}, ...), branch_computations={%region_1.1_spmd, %region_2.2_spmd} | conditional | flops 1083179008 | bytes 39321852 | solution.py:111
  117.4 5.0 %multiply_subtract_fusion = (f32[256,1024]{0,1:T(8,128)S(1)}, f32[256,1024]{0,1:T(8,128)S(1)}, f32[256,1024]{0,1:T(8,128)}, f32[256,1024]{0,1:T(8,128)}) fusion(f32[256,1024]{0,1:T(8,128)} %get-tuple-element.336, f32[256,1024]{0,1:T(8,128)S(1)} %fusion.22, f32[256,1024]{0,1:T(8,128)} %get-tuple-element.335, f32[256,1024]{0,1:T(8,128)} %get-tuple-element.323, ...), kind=kOutput, calls=%fused_computation.31 | convolution fusion | flops 71041024 | bytes 12910600 | tf_op jit(solution)/shard_map/while/body/eval_jaxpr/cond/branch_1_fun/dot_general | solution.py:22
  124.4 2.6 %fusion.20 = f32[640,1024]{0,1:T(8,128)} fusion(f32[640,1024]{0,1:T(8,128)} %get-tuple-element.334, s32[]{:T(128)S(6)} %select_n.24, f32[1024,256]{1,0:T(8,128)S(1)} %convolution_add_fusion.2, f32[1024,256]{1,0:T(8,128)S(1)} %convolution_add_fusion.1, bf16[256,256]{1,0:T(8,128)(2,1)S(1)} %copy-done.2, f32[256,1024]{0,1:T(8,128)S(1)} %get-tuple-element.545), kind=kOutput, calls=%fused_computation.13 | convolution fusion | flops 135528448 | bytes 5373956 | tf_op jit(solution)/shard_map/while/body/eval_jaxpr/cond/branch_1_fun/dot_general | solution.py:32
  127.0 1.9 %subtract_convert_fusion.25 = (bf16[256,256]{1,0:T(8,128)(2,1)}, bf16[256,256]{1,0:T(8,128)(2,1)}, bf16[256,256]{1,0:T(8,128)(2,1)S(1)}, bf16[256,256]{1,0:T(8,128)(2,1)}) fusion(s32[256]{0:T(256)S(1)} %get-tuple-element.688), kind=kLoop, calls=%fused_computation.62.clone.1 | loop fusion | flops 1441792 | bytes 525312 | tf_op jit(solution)/shard_map/convert_element_type | solution.py:9
  131.2 13.4 %conditional.5 = ((f32[256,1024]{0,1:T(8,128)}, f32[256,1024]{0,1:T(8,128)}, f32[640,1024]{0,1:T(8,128)})) conditional(s32[]{:T(128)} %convert_element_type.670, (f32[256,1024]{0,1:T(8,128)}, f32[256,1024]{0,1:T(8,128)}, f32[640,1024]{0,1:T(8,128)}) %tuple.73, (s32[]{:T(128)}, bf16[4,128,1024]{2,1,0:T(8,128)(2,1)}, bf16[256,128]{1,0:T(8,128)(2,1)}, ...), branch_computations={%region_1.1_spmd, %region_2.2_spmd} | conditional | flops 1083179008 | bytes 39321852 | solution.py:111
  135.1 5.0 %multiply_subtract_fusion = (f32[256,1024]{0,1:T(8,128)S(1)}, f32[256,1024]{0,1:T(8,128)S(1)}, f32[256,1024]{0,1:T(8,128)}, f32[256,1024]{0,1:T(8,128)}) fusion(f32[256,1024]{0,1:T(8,128)} %get-tuple-element.336, f32[256,1024]{0,1:T(8,128)S(1)} %fusion.22, f32[256,1024]{0,1:T(8,128)} %get-tuple-element.335, f32[256,1024]{0,1:T(8,128)} %get-tuple-element.323, ...), kind=kOutput, calls=%fused_computation.31 | convolution fusion | flops 71041024 | bytes 12910600 | tf_op jit(solution)/shard_map/while/body/eval_jaxpr/cond/branch_1_fun/dot_general | solution.py:22
  142.0 2.6 %fusion.20 = f32[640,1024]{0,1:T(8,128)} fusion(f32[640,1024]{0,1:T(8,128)} %get-tuple-element.334, s32[]{:T(128)S(6)} %select_n.24, f32[1024,256]{1,0:T(8,128)S(1)} %convolution_add_fusion.2, f32[1024,256]{1,0:T(8,128)S(1)} %convolution_add_fusion.1, bf16[256,256]{1,0:T(8,128)(2,1)S(1)} %copy-done.2, f32[256,1024]{0,1:T(8,128)S(1)} %get-tuple-element.545), kind=kOutput, calls=%fused_computation.13 | convolution fusion | flops 135528448 | bytes 5373956 | tf_op jit(solution)/shard_map/while/body/eval_jaxpr/cond/branch_1_fun/dot_general | solution.py:32
  144.7 2.0 %copy.14 = bf16[640,1024]{1,0:T(8,128)(2,1)S(1)} copy(f32[640,1024]{0,1:T(8,128)} %get-tuple-element.374) | data formatting | bytes 3932160 | tf_op jit(solution)/shard_map/while | solution.py:113
  147.7 2.0 %fusion.131 = f32[128,1024]{1,0:T(8,128)S(1)} fusion(s32[128]{0:T(128)S(1)} %iota_add_fusion.1, f32[256,1024]{0,1:T(8,128)} %get-tuple-element.373), kind=kOutput, calls=%fused_computation.158 | convolution fusion | flops 67862528 | bytes 1573376 | tf_op jit(solution)/shard_map/dot_general | solution.py:30
  149.7 2.0 %fusion.135 = f32[128,1024]{1,0:T(8,128)S(1)} fusion(s32[128]{0:T(128)S(1)} %iota_add_fusion.1, f32[256,1024]{0,1:T(8,128)} %get-tuple-element.372), kind=kOutput, calls=%fused_computation.159 | convolution fusion | flops 67862528 | bytes 1573376 | tf_op jit(solution)/shard_map/dot_general | solution.py:30
  151.7 2.3 %convolution_add_fusion.9 = f32[128,1024]{1,0:T(8,128)S(1)} fusion(f32[128,1024]{1,0:T(8,128)S(1)} %fusion.131, f32[256,1024]{0,1:T(8,128)} %get-tuple-element.373, s32[128]{0:T(128)S(1)} %iota_add_fusion.1), kind=kOutput, calls=%fused_computation.98 | convolution fusion | flops 68780032 | bytes 2097664 | tf_op jit(solution)/shard_map/dot_general | solution.py:31
  154.0 2.3 %convolution_add_fusion.11 = f32[128,1024]{1,0:T(8,128)S(1)} fusion(f32[128,1024]{1,0:T(8,128)S(1)} %fusion.135, f32[256,1024]{0,1:T(8,128)} %get-tuple-element.372, s32[128]{0:T(128)S(1)} %iota_add_fusion.1), kind=kOutput, calls=%fused_computation.100 | convolution fusion | flops 68780032 | bytes 2097664 | tf_op jit(solution)/shard_map/dot_general | solution.py:31
  156.3 2.0 %convolution_add_fusion.10 = f32[128,1024]{1,0:T(8,128)S(1)} fusion(f32[128,1024]{1,0:T(8,128)S(1)} %convolution_add_fusion.11, s32[128]{0:T(128)S(1)} %iota_add_fusion.1, f32[256,1024]{0,1:T(8,128)} %get-tuple-element.372), kind=kOutput, calls=%fused_computation.99 | convolution fusion | flops 68091904 | bytes 2097664 | tf_op jit(solution)/shard_map/dot_general | solution.py:32
  158.3 2.7 %fusion.74 = bf16[128,1024]{1,0:T(8,128)(2,1)} fusion(f32[128,1024]{1,0:T(8,128)S(1)} %convolution_add_fusion.10, f32[128,1024]{1,0:T(8,128)S(1)} %convolution_add_fusion.9, bf16[128,1024]{1,0:T(8,128)(2,1)S(1)} %copy-done.5, f32[1024]{0:T(1024)S(1)} %copy-done.6, s32[128]{0:T(128)S(1)} %iota_add_fusion.1, f32[256,1024]{0,1:T(8,128)} %get-tuple-element.373), kind=kOutput, calls=%fused_computation.101 | convolution fusion | flops 68878336 | bytes 2626048 | tf_op jit(solution)/shard_map/dot_general | solution.py:32
  161.0 12.1 %reduce-scatter.2.cloned.1.call-done = bf16[128,1024]{1,0:T(8,128)(2,1)} async-done(((bf16[512,1024]{1,0:T(8,128)(2,1)}), bf16[128,1024]{1,0:T(8,128)(2,1)}) %reduce-scatter.2.cloned.1.call-update) | async-done | bytes 262160 | tf_op jit(solution)/shard_map/reduce_scatter | solution.py:118
  173.2 1.8 convert_element_type.265
  (94 shorter events, 47.9 us)
Async XLA Ops:
  7.2 2.7 %copy-start = (bf16[128,1024]{1,0:T(8,128)(2,1)S(1)}, bf16[128,1024]{1,0:T(8,128)(2,1)}, u32[]{:S(2)}) copy-start(bf16[128,1024]{1,0:T(8,128)(2,1)} %param.11) | copy-start | bytes 786436
  7.2 33.1 %all-gather.4.cloned.1.call-start = ((), (), s32[]{:S(2)}) async-start(), calls=%async_computation.1 | async-start | bytes 1310720 | tf_op jit(solution)/shard_map/all_gather | solution.py:72
  7.9 62.1 %all-gather.6.cloned.1.call-start = ((), (), s32[]{:S(2)}) async-start(), calls=%async_computation.3 | async-start | bytes 1310720 | tf_op jit(solution)/shard_map/all_gather | solution.py:99
  9.8 163.4 %reduce-scatter.2.cloned.1.call-start = ((), (), s32[]{:S(2)}) async-start(), calls=%async_computation.2 | async-start | bytes 1310720 | tf_op jit(solution)/shard_map/reduce_scatter | solution.py:118
  40.2 2.2 %copy-start.4 = (bf16[512,1024]{1,0:T(8,128)(2,1)S(1)}, bf16[512,1024]{1,0:T(8,128)(2,1)}, u32[]{:S(2)}) copy-start(bf16[512,1024]{1,0:T(8,128)(2,1)} %all-gather.4.cloned.1.call-done) | copy-start | bytes 3145732
  87.0 0.9 copy-start.1
  87.3 1.3 copy-start.3
  87.9 1.0 copy-start.2
  104.7 0.9 copy-start.1
  105.0 1.2 copy-start.3
  105.6 1.0 copy-start.2
  122.4 0.9 copy-start.1
  122.8 1.2 copy-start.3
  123.3 1.0 copy-start.2
  140.1 0.9 copy-start.1
  140.4 1.3 copy-start.3
  141.0 1.0 copy-start.2
  149.7 8.6 %copy-start.5 = (bf16[128,1024]{1,0:T(8,128)(2,1)S(1)}, bf16[128,1024]{1,0:T(8,128)(2,1)}, u32[]{:S(2)}) copy-start(bf16[128,1024]{1,0:T(8,128)(2,1)} %multiply_convert_fusion) | copy-start | bytes 786436
  149.7 8.6 %copy-start.6 = (f32[1024]{0:T(1024)S(1)}, f32[1024]{0:T(1024)}, u32[]{:S(2)}) copy-start(f32[1024]{0:T(1024)} %param.13) | copy-start | bytes 12292
Sparse Core Ops, SparseCore 0:
  9.6 30.6 all-gather.3
  42.4 27.5 all-gather.5
  147.8 25.2 reduce-scatter.1
where the time goes:
time: 182 us; the launch traced here: 181 us
  matrix products  79.1 us (43%)
  waiting for transfers between devices  54 us (30%)
  other arithmetic  20.7 us (11%)
  between operations  13.9 us (8%)
  local copies, waits for them, and re-layouts  13.3 us (7%)
    dot_general x10, matrix products, table_times(): jnp.dot(low_part, signal, preferred_element_type=jnp.float32)  26.5 us
    all_gather x1, waiting for transfers between devices, shards(): taps = lax.all_gather(filter_taps, 'ctx', axis=0, tiled=True)  24.8 us
    dot_general x10, matrix products, table_times_float(): jnp.dot(low_part, value_high, preferred_element_type=jnp.float32)  16.6 us
    all_gather x1, waiting for transfers between devices, shards(): spans = lax.all_gather(grad_y[None], 'ctx', axis=0, tiled=True)  16.3 us
    convert_element_type x8, other arithmetic, split_parts(): low_part = (values - high_part.astype(jnp.float32)).astype(jnp.bfloat16)  12.4 us
    reduce_scatter x1, waiting for transfers between devices, shards(): lax.psum_scatter(lag_sums[span_len:].astype(jnp.bfloat16), 'ctx', scatter...  12.1 us
    dot_general x10, matrix products, table_times(): jnp.dot(high_part, signal, preferred_element_type=jnp.float32)  11.6 us
    dot_general x10, matrix products, table_times_float(): jnp.dot(high_part, value_low, preferred_element_type=jnp.float32)  7.3 us
  transfers between devices with their start and end apart: 3, of which 3 were waited for; matrix products, arithmetic and copies ran while one was open for 19% of the time, Pallas kernels for 0%

commit v1 on v0

v1 whole, which is shorter than its diff:
```python
import functools

import jax
import jax.numpy as jnp
import ml_dtypes
import numpy as np
from jax import lax
from jax.sharding import PartitionSpec as P


@functools.cache
def tables(seq):
    bins = np.arange(seq)[:, None] * 2 + 1
    places = np.arange(seq)[None, :]
    angles = (bins * places % (4 * seq)) * (np.pi / (2 * seq))
    forward = np.concatenate([np.cos(angles), np.sin(angles)], axis=0)
    inverse = np.concatenate([np.cos(angles), np.sin(angles)], axis=0).T / seq
    return forward.astype(ml_dtypes.bfloat16), inverse.astype(ml_dtypes.bfloat16)


def shards(grad_out, gate_act, conv_input, filter_taps, skip_gain):
    span, channels = grad_out.shape
    parts = lax.axis_size("ctx")
    own = lax.axis_index("ctx")
    seq = span * parts
    width = channels // parts
    forward, inverse = tables(seq)
    shifts = sorted(range(1, parts), key=lambda s: (abs(2 * s - parts), s))

    def moved(piece, shift):
        return lax.ppermute(piece, "ctx", [(i, (i + shift) % parts) for i in range(parts)])

    def scatter(values):
        pieces = [None] * parts
        pieces[0] = lax.dynamic_slice_in_dim(values, own * width, width, 1)
        for shift in shifts:
            target = (own + shift) % parts
            pieces[parts - shift] = moved(
                lax.dynamic_slice_in_dim(values, target * width, width, 1), shift
            )
        ahead = jnp.concatenate(pieces + pieces, axis=0)
        return lax.dynamic_slice_in_dim(ahead, (parts - own) % parts * span, seq, 0)

    def gather(values):
        pieces = [None] * parts
        pieces[0] = lax.dynamic_slice_in_dim(values, own * span, span, 0)
        for shift in shifts:
            target = (own + shift) % parts
            pieces[parts - shift] = moved(
                lax.dynamic_slice_in_dim(values, target * span, span, 0), shift
            )
        ahead = jnp.concatenate(pieces + pieces, axis=1)
        return lax.dynamic_slice_in_dim(ahead, (parts - own) % parts * width, channels, 1)

    def spectrum(signal):
        both = jnp.dot(forward, signal, preferred_element_type=jnp.float32)
        return both[:seq], both[seq:]

    def correlate(first, second):
        real = first[0] * second[0] + first[1] * second[1]
        imag = first[1] * second[0] - first[0] * second[1]
        both = jnp.concatenate([real, imag], axis=0).astype(jnp.bfloat16)
        return jnp.dot(inverse, both, preferred_element_type=jnp.float32)

    grad_y = (grad_out.astype(jnp.float32) * gate_act.astype(jnp.float32)).astype(jnp.bfloat16)
    taps = scatter(filter_taps)
    grads = scatter(grad_y)
    inputs = scatter(conv_input)
    gain = lax.dynamic_slice_in_dim(skip_gain, own * width, width, 0)
    grad_spec = spectrum(grads)
    conv_part = correlate(grad_spec, spectrum(taps))
    grad_input = (conv_part + gain[None, :] * grads.astype(jnp.float32)).astype(jnp.bfloat16)
    grad_input = gather(grad_input)
    grad_filter = gather(correlate(grad_spec, spectrum(inputs)).astype(jnp.bfloat16))
    return grad_input, grad_filter.astype(jnp.float32)


def solution(mesh):
    return jax.shard_map(
        shards,
        mesh=mesh,
        in_specs=(
            P(("grp", "ctx"), "chan"),
            P(("grp", "ctx"), "chan"),
            P(("grp", "ctx"), "chan"),
            P("ctx", "chan"),
            P("chan"),
        ),
        out_specs=(P(("grp", "ctx"), "chan"), P(("grp", "ctx"), "chan")),
        check_vma=False,
    )
```

time: 182 us -> 40.4 us (0.22)
  matrix products: 79.1 us -> 2.81 us
  waiting for transfers between devices: 54 us -> 5.4 us
  starting transfers between devices: 0.12 us -> 24 us
  other arithmetic: 20.7 us -> 0.12 us
  between operations: 13.9 us -> 1.08 us
  local copies, waits for them, and re-layouts: 13.3 us -> 6.71 us
    dot_general x54 -> x7, matrix products: 79.1 us -> 2.81 us  [the longest x4 1.45 us: correlate(): return jnp.dot(inverse, both, preferred_element_type=jnp.float32)]
    all_gather x2 -> x0, waiting for transfers between devices: 41.1 us -> none  [the longest x1 24.8 us: shards(): taps = lax.all_gather(filter_taps, 'ctx', axis=0, tiled=True)]
    ppermute x0 -> x15, starting transfers between devices: none -> 24 us  [moved(): lax.ppermute(piece, 'ctx', [(i, (i + shift) % parts) for i in range(parts)])]
    convert_element_type x13 -> x1, other arithmetic: 18.9 us -> 0.04 us  [shards(): return (grad_input, grad_filter.astype(jnp.float32))]
    reduce_scatter x1 -> x0, waiting for transfers between devices: 12.1 us -> none  [shards(): lax.psum_scatter(lag_sums[span_len:].astype(jnp.bfloat16), 'ctx', scatter...]
    ppermute x0 -> x15, waiting for transfers between devices: none -> 5.4 us  [moved(): lax.ppermute(piece, 'ctx', [(i, (i + shift) % parts) for i in range(parts)])]
    broadcast_in_dim x3 -> x0, local copies, waits for them, and re-layouts: 3.84 us -> none  [the longest x2 2.1 us: shards(): zero_spec = jnp.zeros((period, channels), jnp.float32)]
    slice x2 -> x0, local copies, waits for them, and re-layouts: 2.39 us -> none  [the longest x1 1.34 us: shards(): taps_padded[:-span_len].reshape(cycle_size, span_len, channels)]
  transfers between devices with their start and end apart: 3 -> 15, of which waited for: 3 -> 6; matrix products, arithmetic and copies ran while one was open for 19% -> 16% of each run, Pallas kernels for 0% -> 0%
where the time goes in v1:
time: 40.4 us; the launch traced here: 40.1 us
  starting transfers between devices  24 us (59%)
  local copies, waits for them, and re-layouts  6.71 us (17%)
  waiting for transfers between devices  5.4 us (13%)
  matrix products  2.81 us (7%)
  between operations  1.08 us (3%)
    ppermute x15, starting transfers between devices, moved(): lax.ppermute(piece, 'ctx', [(i, (i + shift) % parts) for i in range(parts)])  24 us
    ppermute x15, waiting for transfers between devices, moved(): lax.ppermute(piece, 'ctx', [(i, (i + shift) % parts) for i in range(parts)])  5.4 us
    unnamed x47, local copies, waits for them, and re-layouts  4.68 us
    dot_general x4, matrix products, correlate(): return jnp.dot(inverse, both, preferred_element_type=jnp.float32)  1.45 us
    dot_general x3, matrix products, spectrum(): both = jnp.dot(forward, signal, preferred_element_type=jnp.float32)  1.35 us
    dynamic_slice x3, local copies, waits for them, and re-layouts, scatter(): lax.dynamic_slice_in_dim(values, target * width, width, 1)  1.08 us
  transfers between devices with their start and end apart: 15, of which 6 were waited for; matrix products, arithmetic and copies ran while one was open for 16% of the time, Pallas kernels for 0%

profile of v1, /device:TPU:0, one launch (start us, length us, event | category | flops | bytes accessed | tf_op | source)
XLA Modules:
  0.0 40.1 jit_solution(17768895667539156528)
XLA Ops:
  0.7 1.0 %constant_dynamic-slice_fusion.7 = (bf16[128,256]{1,0:T(8,128)(2,1)S(1)}, bf16[1024,256]{1,0:T(8,128)(2,1)S(1)}, bf16[128,256]{1,0:T(8,128)(2,1)S(1)}, bf16[128,256]{1,0:T(8,128)(2,1)S(1)}) fusion(bf16[128,1024]{1,0:T(8,128)(2,1)} %param.10, s32[]{:T(128)S(6)} %select_n.103, s32[]{:T(128)S(6)} %select_n.97, s32[]{:T(128)S(6)} %select_n.99, s32[]{:T(128)S(6)} %select_n.101), kind=kLoop, calls=%fused_computation.71 | loop fusion | bytes 524304 | tf_op jit(solution)/shard_map/dynamic_slice | solution.py:39
  1.7 5.1 %collective-permute-start.3 = (bf16[128,256]{1,0:T(8,128)(2,1)S(1)}, bf16[128,256]{1,0:T(8,128)(2,1)S(1)}, u32[]{:S(2)}, u32[]{:S(2)}) collective-permute-start(bf16[128,256]{1,0:T(8,128)(2,1)S(1)} %get-tuple-element.21), channel_id=1, source_target_pairs={{0,12},{4,0},{8,4},{12,8},{1,13},{5,1},{9,5},{13,9},{2,14},{6,2},{... | collective-permute-start | bytes 196616 | tf_op jit(solution)/shard_map/ppermute | solution.py:31
  6.8 1.0 %collective-permute-start.5 = (bf16[128,256]{1,0:T(8,128)(2,1)S(1)}, bf16[128,256]{1,0:T(8,128)(2,1)S(1)}, u32[]{:S(2)}, u32[]{:S(2)}) collective-permute-start(bf16[128,256]{1,0:T(8,128)(2,1)S(1)} %get-tuple-element.19), channel_id=1, source_target_pairs={{0,4},{4,8},{8,12},{12,0},{1,5},{5,9},{9,13},{13,1},{2,6},{6,10},{... | collective-permute-start | bytes 196616 | tf_op jit(solution)/shard_map/ppermute | solution.py:31
  8.3 2.9 %collective-permute-start = (bf16[128,256]{0,1:T(8,128)(2,1)S(1)}, bf16[128,256]{0,1:T(8,128)(2,1)S(1)}, u32[]{:S(2)}, u32[]{:S(2)}) collective-permute-start(bf16[128,256]{0,1:T(8,128)(2,1)S(1)} %get-tuple-element.18), channel_id=1, source_target_pairs={{0,12},{4,0},{8,4},{12,8},{1,13},{5,1},{9,5},{13,9},{2,14},{6,2},{... | collective-permute-start | bytes 196616 | tf_op jit(solution)/shard_map/ppermute | solution.py:31
  11.2 1.1 %collective-permute-start.1 = (bf16[128,256]{0,1:T(8,128)(2,1)S(1)}, bf16[128,256]{0,1:T(8,128)(2,1)S(1)}, u32[]{:S(2)}, u32[]{:S(2)}) collective-permute-start(bf16[128,256]{0,1:T(8,128)(2,1)S(1)} %get-tuple-element.17), channel_id=1, source_target_pairs={{0,8},{4,12},{8,0},{12,4},{1,9},{5,13},{9,1},{13,5},{2,10},{6,14},... | collective-permute-start | bytes 196616 | tf_op jit(solution)/shard_map/ppermute | solution.py:31
  12.3 0.8 %dynamic_slice.88 = f32[256]{0:T(256)S(1)} dynamic-slice(f32[1024]{0:T(1024)} %param.11, s32[]{:T(128)S(6)} %select_n.97), dynamic_slice_sizes={256} | dynamic-slice | bytes 2052 | tf_op jit(solution)/shard_map/dynamic_slice | solution.py:69
  13.1 0.8 %collective-permute-start.2 = (bf16[128,256]{0,1:T(8,128)(2,1)S(1)}, bf16[128,256]{0,1:T(8,128)(2,1)S(1)}, u32[]{:S(2)}, u32[]{:S(2)}) collective-permute-start(bf16[128,256]{0,1:T(8,128)(2,1)S(1)} %get-tuple-element.15), channel_id=1, source_target_pairs={{0,4},{4,8},{8,12},{12,0},{1,5},{5,9},{9,13},{13,1},{2,6},{6,10},{... | collective-permute-start | bytes 196616 | tf_op jit(solution)/shard_map/ppermute | solution.py:31
  13.9 0.2 collective-permute-done.4
  14.2 2.9 %collective-permute-start.9 = (bf16[128,256]{1,0:T(8,128)(2,1)S(1)}, bf16[128,256]{1,0:T(8,128)(2,1)S(1)}, u32[]{:S(2)}, u32[]{:S(2)}) collective-permute-start(bf16[128,256]{1,0:T(8,128)(2,1)S(1)} %get-tuple-element.9), channel_id=1, source_target_pairs={{0,12},{4,0},{8,4},{12,8},{1,13},{5,1},{9,5},{13,9},{2,14},{6,2},{... | collective-permute-start | bytes 196616 | tf_op jit(solution)/shard_map/ppermute | solution.py:31
  17.1 1.4 %collective-permute-start.10 = (bf16[128,256]{1,0:T(8,128)(2,1)S(1)}, bf16[128,256]{1,0:T(8,128)(2,1)S(1)}, u32[]{:S(2)}, u32[]{:S(2)}) collective-permute-start(bf16[128,256]{1,0:T(8,128)(2,1)S(1)} %get-tuple-element.10), channel_id=1, source_target_pairs={{0,8},{4,12},{8,0},{12,4},{1,9},{5,13},{9,1},{13,5},{2,10},{6,14},... | collective-permute-start | bytes 196616 | tf_op jit(solution)/shard_map/ppermute | solution.py:31
  18.5 0.8 %constant_dynamic-update-slice_fusion.11 = bf16[1024,256]{1,0:T(8,128)(2,1)S(1)} fusion(bf16[1024,256]{1,0:T(8,128)(2,1)S(1)} %constant_dynamic-update-slice_fusion.12, bf16[128,1024]{1,0:T(8,128)(2,1)} %param.10, s32[]{:T(128)S(6)} %select_n.97), kind=kLoop, calls=%fused_computation.30 | loop fusion | bytes 131076
  19.4 0.6 %collective-permute-done.1 = bf16[128,256]{0,1:T(8,128)(2,1)S(1)} collective-permute-done((bf16[128,256]{0,1:T(8,128)(2,1)S(1)}, bf16[128,256]{0,1:T(8,128)(2,1)S(1)}, u32[]{:S(2)}, u32[]{:S(2)}) %collective-permute-start.1) | collective-permute-done | bytes 65568 | tf_op jit(solution)/shard_map/ppermute | solution.py:31
  20.1 0.4 %fusion.4 = f32[1024,256]{1,0:T(8,128)S(1)} fusion(bf16[1024,512]{1,0:T(8,128)(2,1)S(1)} %copy-done, bf16[1024,256]{1,0:T(8,128)(2,1)S(1)} %constant_dynamic-update-slice_fusion.8, s32[]{:T(128)S(6)} %select_n.105), kind=kOutput, calls=%fused_computation.13 | convolution fusion | flops 268435456 | bytes 2359300 | tf_op jit(solution)/shard_map/dot_general | solution.py:56
  20.7 0.5 %fusion.8 = f32[1024,256]{1,0:T(8,128)S(1)} fusion(bf16[1024,512]{1,0:T(8,128)(2,1)S(1)} %copy-done, bf16[1024,256]{0,1:T(8,128)(2,1)S(1)} %constant_dynamic-update-slice_fusion, s32[]{:T(128)S(6)} %select_n.105), kind=kOutput, calls=%fused_computation.17 | convolution fusion | flops 268435456 | bytes 2359300 | tf_op jit(solution)/shard_map/dot_general | solution.py:56
  21.1 0.6 %copy-done.2 = bf16[512,512]{1,0:T(8,128)(2,1)S(1)} copy-done((bf16[512,512]{1,0:T(8,128)(2,1)S(1)}, bf16[512,512]{1,0:T(8,128)(2,1)}, u32[]{:S(2)}) %copy-start.2) | copy-done | bytes 524312
  21.7 0.4 fusion.6
  22.1 0.7 %copy-done.1 = bf16[512,512]{1,0:T(8,128)(2,1)S(1)} copy-done((bf16[512,512]{1,0:T(8,128)(2,1)S(1)}, bf16[512,512]{1,0:T(8,128)(2,1)}, u32[]{:S(2)}) %copy-start.1) | copy-done | bytes 524312
  22.7 0.4 add_convert_fusion.1
  23.2 3.3 %collective-permute-start.6 = (bf16[128,256]{0,1:T(8,128)(2,1)S(1)}, bf16[128,256]{0,1:T(8,128)(2,1)S(1)}, u32[]{:S(2)}, u32[]{:S(2)}) collective-permute-start(bf16[128,256]{0,1:T(8,128)(2,1)S(1)} %get-tuple-element.14), channel_id=1, source_target_pairs={{0,12},{4,0},{8,4},{12,8},{1,13},{5,1},{9,5},{13,9},{2,14},{6,2},{... | collective-permute-start | bytes 196616 | tf_op jit(solution)/shard_map/ppermute | solution.py:31
  26.5 1.0 %collective-permute-start.7 = (bf16[128,256]{0,1:T(8,128)(2,1)S(1)}, bf16[128,256]{0,1:T(8,128)(2,1)S(1)}, u32[]{:S(2)}, u32[]{:S(2)}) collective-permute-start(bf16[128,256]{0,1:T(8,128)(2,1)S(1)} %get-tuple-element.13), channel_id=1, source_target_pairs={{0,8},{4,12},{8,0},{12,4},{1,9},{5,13},{9,1},{13,5},{2,10},{6,14},... | collective-permute-start | bytes 196616 | tf_op jit(solution)/shard_map/ppermute | solution.py:31
  27.4 1.9 %collective-permute-start.8 = (bf16[128,256]{0,1:T(8,128)(2,1)S(1)}, bf16[128,256]{0,1:T(8,128)(2,1)S(1)}, u32[]{:S(2)}, u32[]{:S(2)}) collective-permute-start(bf16[128,256]{0,1:T(8,128)(2,1)S(1)} %get-tuple-element.11), channel_id=1, source_target_pairs={{0,4},{4,8},{8,12},{12,0},{1,5},{5,9},{9,13},{13,1},{2,6},{6,10},{... | collective-permute-start | bytes 196616 | tf_op jit(solution)/shard_map/ppermute | solution.py:31
  29.5 0.4 %fusion.2 = f32[1024,256]{1,0:T(8,128)S(1)} fusion(bf16[1024,512]{1,0:T(8,128)(2,1)S(1)} %copy-done, bf16[1024,256]{1,0:T(8,128)(2,1)S(1)} %constant_dynamic-update-slice_fusion.24, s32[]{:T(128)S(6)} %select_n.105), kind=kOutput, calls=%fused_computation.11 | convolution fusion | flops 268435456 | bytes 2359300 | tf_op jit(solution)/shard_map/dot_general | solution.py:56
  29.9 0.4 fusion.7
  30.3 0.4 fusion.1
  30.7 1.9 %collective-permute-start.12 = (bf16[128,256]{0,1:T(8,128)(2,1)S(1)}, bf16[128,256]{0,1:T(8,128)(2,1)S(1)}, u32[]{:S(2)}, u32[]{:S(2)}) collective-permute-start(bf16[128,256]{0,1:T(8,128)(2,1)S(1)} %get-tuple-element.6), channel_id=1, source_target_pairs={{0,12},{4,0},{8,4},{12,8},{1,13},{5,1},{9,5},{13,9},{2,14},{6,2},{... | collective-permute-start | bytes 196616 | tf_op jit(solution)/shard_map/ppermute | solution.py:31
  32.8 0.5 %collective-permute-start.14 = (bf16[128,256]{0,1:T(8,128)(2,1)S(1)}, bf16[128,256]{0,1:T(8,128)(2,1)S(1)}, u32[]{:S(2)}, u32[]{:S(2)}) collective-permute-start(bf16[128,256]{0,1:T(8,128)(2,1)S(1)} %get-tuple-element.4), channel_id=1, source_target_pairs={{0,4},{4,8},{8,12},{12,0},{1,5},{5,9},{9,13},{13,1},{2,6},{6,10},{... | collective-permute-start | bytes 196616 | tf_op jit(solution)/shard_map/ppermute | solution.py:31
  33.4 0.6 %collective-permute-done.8 = bf16[128,256]{0,1:T(8,128)(2,1)S(1)} collective-permute-done((bf16[128,256]{0,1:T(8,128)(2,1)S(1)}, bf16[128,256]{0,1:T(8,128)(2,1)S(1)}, u32[]{:S(2)}, u32[]{:S(2)}) %collective-permute-start.8) | collective-permute-done | bytes 65568 | tf_op jit(solution)/shard_map/ppermute | solution.py:31
  34.2 0.9 %copy.11 = bf16[128,1024]{1,0:T(8,128)(2,1)} copy(bf16[128,1024]{0,1:T(8,128)(2,1)S(1)} %constant_dynamic-slice_fusion.3) | data formatting | bytes 524288
  35.0 0.9 %collective-permute-done.12 = bf16[128,256]{0,1:T(8,128)(2,1)S(1)} collective-permute-done((bf16[128,256]{0,1:T(8,128)(2,1)S(1)}, bf16[128,256]{0,1:T(8,128)(2,1)S(1)}, u32[]{:S(2)}, u32[]{:S(2)}) %collective-permute-start.12) | collective-permute-done | bytes 65568 | tf_op jit(solution)/shard_map/ppermute | solution.py:31
  36.0 2.1 %collective-permute-done.13 = bf16[128,256]{0,1:T(8,128)(2,1)S(1)} collective-permute-done((bf16[128,256]{0,1:T(8,128)(2,1)S(1)}, bf16[128,256]{0,1:T(8,128)(2,1)S(1)}, u32[]{:S(2)}, u32[]{:S(2)}) %collective-permute-start.13) | collective-permute-done | bytes 65568 | tf_op jit(solution)/shard_map/ppermute | solution.py:31
  38.1 0.8 %collective-permute-done.14 = bf16[128,256]{0,1:T(8,128)(2,1)S(1)} collective-permute-done((bf16[128,256]{0,1:T(8,128)(2,1)S(1)}, bf16[128,256]{0,1:T(8,128)(2,1)S(1)}, u32[]{:S(2)}, u32[]{:S(2)}) %collective-permute-start.14) | collective-permute-done | bytes 65568 | tf_op jit(solution)/shard_map/ppermute | solution.py:31
  39.1 1.0 %copy.12 = f32[128,1024]{1,0:T(8,128)} copy(f32[128,1024]{0,1:T(8,128)S(1)} %dynamic-slice_convert_fusion) | data formatting | bytes 1048576
  (66 shorter events, 1.3 us)
Async XLA Ops:
  0.7 7.1 %copy-start.4 = (bf16[128,1024]{1,0:T(8,128)(2,1)S(1)}, bf16[128,1024]{1,0:T(8,128)(2,1)}, u32[]{:S(2)}) copy-start(bf16[128,1024]{1,0:T(8,128)(2,1)} %param.8) | copy-start | bytes 786436
  1.7 11.4 %collective-permute-start.3 = (bf16[128,256]{1,0:T(8,128)(2,1)S(1)}, bf16[128,256]{1,0:T(8,128)(2,1)S(1)}, u32[]{:S(2)}, u32[]{:S(2)}) collective-permute-start(bf16[128,256]{1,0:T(8,128)(2,1)S(1)} %get-tuple-element.21), channel_id=1, source_target_pairs={{0,12},{4,0},{8,4},{12,8},{1,13},{5,1},{9,5},{13,9},{2,14},{6,2},{... | collective-permute-start | bytes 196616 | tf_op jit(solution)/shard_map/ppermute | solution.py:31
  6.8 7.4 %collective-permute-start.4 = (bf16[128,256]{1,0:T(8,128)(2,1)S(1)}, bf16[128,256]{1,0:T(8,128)(2,1)S(1)}, u32[]{:S(2)}, u32[]{:S(2)}) collective-permute-start(bf16[128,256]{1,0:T(8,128)(2,1)S(1)} %get-tuple-element.22), channel_id=1, source_target_pairs={{0,8},{4,12},{8,0},{12,4},{1,9},{5,13},{9,1},{13,5},{2,10},{6,14},... | collective-permute-start | bytes 196616 | tf_op jit(solution)/shard_map/ppermute | solution.py:31
  6.8 1.2 %copy-start.5 = (bf16[128,1024]{1,0:T(8,128)(2,1)S(1)}, bf16[128,1024]{1,0:T(8,128)(2,1)}, u32[]{:S(2)}) copy-start(bf16[128,1024]{1,0:T(8,128)(2,1)} %param.7) | copy-start | bytes 786436
  6.8 10.3 %collective-permute-start.5 = (bf16[128,256]{1,0:T(8,128)(2,1)S(1)}, bf16[128,256]{1,0:T(8,128)(2,1)S(1)}, u32[]{:S(2)}, u32[]{:S(2)}) collective-permute-start(bf16[128,256]{1,0:T(8,128)(2,1)S(1)} %get-tuple-element.19), channel_id=1, source_target_pairs={{0,4},{4,8},{8,12},{12,0},{1,5},{5,9},{9,13},{13,1},{2,6},{6,10},{... | collective-permute-start | bytes 196616 | tf_op jit(solution)/shard_map/ppermute | solution.py:31
  8.3 4.8 %copy-start.3 = (bf16[128,1024]{1,0:T(8,128)(2,1)S(1)}, bf16[128,1024]{1,0:T(8,128)(2,1)}, u32[]{:S(2)}) copy-start(bf16[128,1024]{1,0:T(8,128)(2,1)} %param.9) | copy-start | bytes 786436
  8.3 11.8 %copy-start = (bf16[1024,512]{1,0:T(8,128)(2,1)S(1)}, bf16[1024,512]{1,0:T(8,128)(2,1)}, u32[]{:S(2)}) copy-start(bf16[1024,512]{1,0:T(8,128)(2,1)} %constant.82.clone) | copy-start | bytes 3145732
  8.3 11.0 %collective-permute-start = (bf16[128,256]{0,1:T(8,128)(2,1)S(1)}, bf16[128,256]{0,1:T(8,128)(2,1)S(1)}, u32[]{:S(2)}, u32[]{:S(2)}) collective-permute-start(bf16[128,256]{0,1:T(8,128)(2,1)S(1)} %get-tuple-element.18), channel_id=1, source_target_pairs={{0,12},{4,0},{8,4},{12,8},{1,13},{5,1},{9,5},{13,9},{2,14},{6,2},{... | collective-permute-start | bytes 196616 | tf_op jit(solution)/shard_map/ppermute | solution.py:31
  11.2 8.8 %collective-permute-start.1 = (bf16[128,256]{0,1:T(8,128)(2,1)S(1)}, bf16[128,256]{0,1:T(8,128)(2,1)S(1)}, u32[]{:S(2)}, u32[]{:S(2)}) collective-permute-start(bf16[128,256]{0,1:T(8,128)(2,1)S(1)} %get-tuple-element.17), channel_id=1, source_target_pairs={{0,8},{4,12},{8,0},{12,4},{1,9},{5,13},{9,1},{13,5},{2,10},{6,14},... | collective-permute-start | bytes 196616 | tf_op jit(solution)/shard_map/ppermute | solution.py:31
  13.1 6.9 %collective-permute-start.2 = (bf16[128,256]{0,1:T(8,128)(2,1)S(1)}, bf16[128,256]{0,1:T(8,128)(2,1)S(1)}, u32[]{:S(2)}, u32[]{:S(2)}) collective-permute-start(bf16[128,256]{0,1:T(8,128)(2,1)S(1)} %get-tuple-element.15), channel_id=1, source_target_pairs={{0,4},{4,8},{8,12},{12,0},{1,5},{5,9},{9,13},{13,1},{2,6},{6,10},{... | collective-permute-start | bytes 196616 | tf_op jit(solution)/shard_map/ppermute | solution.py:31
  14.2 13.2 %collective-permute-start.9 = (bf16[128,256]{1,0:T(8,128)(2,1)S(1)}, bf16[128,256]{1,0:T(8,128)(2,1)S(1)}, u32[]{:S(2)}, u32[]{:S(2)}) collective-permute-start(bf16[128,256]{1,0:T(8,128)(2,1)S(1)} %get-tuple-element.9), channel_id=1, source_target_pairs={{0,12},{4,0},{8,4},{12,8},{1,13},{5,1},{9,5},{13,9},{2,14},{6,2},{... | collective-permute-start | bytes 196616 | tf_op jit(solution)/shard_map/ppermute | solution.py:31
  17.1 12.3 %collective-permute-start.10 = (bf16[128,256]{1,0:T(8,128)(2,1)S(1)}, bf16[128,256]{1,0:T(8,128)(2,1)S(1)}, u32[]{:S(2)}, u32[]{:S(2)}) collective-permute-start(bf16[128,256]{1,0:T(8,128)(2,1)S(1)} %get-tuple-element.10), channel_id=1, source_target_pairs={{0,8},{4,12},{8,0},{12,4},{1,9},{5,13},{9,1},{13,5},{2,10},{6,14},... | collective-permute-start | bytes 196616 | tf_op jit(solution)/shard_map/ppermute | solution.py:31
  19.3 10.1 %collective-permute-start.11 = (bf16[128,256]{1,0:T(8,128)(2,1)S(1)}, bf16[128,256]{1,0:T(8,128)(2,1)S(1)}, u32[]{:S(2)}, u32[]{:S(2)}) collective-permute-start(bf16[128,256]{1,0:T(8,128)(2,1)S(1)} %get-tuple-element.7), channel_id=1, source_target_pairs={{0,4},{4,8},{8,12},{12,0},{1,5},{5,9},{9,13},{13,1},{2,6},{6,10},{... | collective-permute-start | bytes 196616 | tf_op jit(solution)/shard_map/ppermute | solution.py:31
  20.6 1.0 %copy-start.2 = (bf16[512,512]{1,0:T(8,128)(2,1)S(1)}, bf16[512,512]{1,0:T(8,128)(2,1)}, u32[]{:S(2)}) copy-start(bf16[512,512]{1,0:T(8,128)(2,1)} %constant.84) | copy-start | bytes 1572868
  21.7 1.0 %copy-start.1 = (bf16[512,512]{1,0:T(8,128)(2,1)S(1)}, bf16[512,512]{1,0:T(8,128)(2,1)}, u32[]{:S(2)}) copy-start(bf16[512,512]{1,0:T(8,128)(2,1)} %constant.85) | copy-start | bytes 1572868
  23.2 9.7 %collective-permute-start.6 = (bf16[128,256]{0,1:T(8,128)(2,1)S(1)}, bf16[128,256]{0,1:T(8,128)(2,1)S(1)}, u32[]{:S(2)}, u32[]{:S(2)}) collective-permute-start(bf16[128,256]{0,1:T(8,128)(2,1)S(1)} %get-tuple-element.14), channel_id=1, source_target_pairs={{0,12},{4,0},{8,4},{12,8},{1,13},{5,1},{9,5},{13,9},{2,14},{6,2},{... | collective-permute-start | bytes 196616 | tf_op jit(solution)/shard_map/ppermute | solution.py:31
  26.5 6.9 %collective-permute-start.7 = (bf16[128,256]{0,1:T(8,128)(2,1)S(1)}, bf16[128,256]{0,1:T(8,128)(2,1)S(1)}, u32[]{:S(2)}, u32[]{:S(2)}) collective-permute-start(bf16[128,256]{0,1:T(8,128)(2,1)S(1)} %get-tuple-element.13), channel_id=1, source_target_pairs={{0,8},{4,12},{8,0},{12,4},{1,9},{5,13},{9,1},{13,5},{2,10},{6,14},... | collective-permute-start | bytes 196616 | tf_op jit(solution)/shard_map/ppermute | solution.py:31
  27.4 6.6 %collective-permute-start.8 = (bf16[128,256]{0,1:T(8,128)(2,1)S(1)}, bf16[128,256]{0,1:T(8,128)(2,1)S(1)}, u32[]{:S(2)}, u32[]{:S(2)}) collective-permute-start(bf16[128,256]{0,1:T(8,128)(2,1)S(1)} %get-tuple-element.11), channel_id=1, source_target_pairs={{0,4},{4,8},{8,12},{12,0},{1,5},{5,9},{9,13},{13,1},{2,6},{6,10},{... | collective-permute-start | bytes 196616 | tf_op jit(solution)/shard_map/ppermute | solution.py:31
  30.7 5.2 %collective-permute-start.12 = (bf16[128,256]{0,1:T(8,128)(2,1)S(1)}, bf16[128,256]{0,1:T(8,128)(2,1)S(1)}, u32[]{:S(2)}, u32[]{:S(2)}) collective-permute-start(bf16[128,256]{0,1:T(8,128)(2,1)S(1)} %get-tuple-element.6), channel_id=1, source_target_pairs={{0,12},{4,0},{8,4},{12,8},{1,13},{5,1},{9,5},{13,9},{2,14},{6,2},{... | collective-permute-start | bytes 196616 | tf_op jit(solution)/shard_map/ppermute | solution.py:31
  32.6 5.5 %collective-permute-start.13 = (bf16[128,256]{0,1:T(8,128)(2,1)S(1)}, bf16[128,256]{0,1:T(8,128)(2,1)S(1)}, u32[]{:S(2)}, u32[]{:S(2)}) collective-permute-start(bf16[128,256]{0,1:T(8,128)(2,1)S(1)} %get-tuple-element.5), channel_id=1, source_target_pairs={{0,8},{4,12},{8,0},{12,4},{1,9},{5,13},{9,1},{13,5},{2,10},{6,14},... | collective-permute-start | bytes 196616 | tf_op jit(solution)/shard_map/ppermute | solution.py:31
  32.8 6.1 %collective-permute-start.14 = (bf16[128,256]{0,1:T(8,128)(2,1)S(1)}, bf16[128,256]{0,1:T(8,128)(2,1)S(1)}, u32[]{:S(2)}, u32[]{:S(2)}) collective-permute-start(bf16[128,256]{0,1:T(8,128)(2,1)S(1)} %get-tuple-element.4), channel_id=1, source_target_pairs={{0,4},{4,8},{8,12},{12,0},{1,5},{5,9},{9,13},{13,1},{2,6},{6,10},{... | collective-permute-start | bytes 196616 | tf_op jit(solution)/shard_map/ppermute | solution.py:31

commit v2 on v1

v2 whole, which is shorter than its diff:
```python
import functools

import jax
import jax.numpy as jnp
import ml_dtypes
import numpy as np
from jax import lax
from jax.experimental import pallas as pl
from jax.experimental.pallas import tpu as pltpu
from jax.sharding import PartitionSpec as P

KIB = 1 << 10
CHUNKS = 8
ORDER = (1, 2, 3)


@functools.cache
def tables(seq):
    bins = np.arange(seq)[:, None] * 2 + 1
    places = np.arange(seq)[None, :]
    angles = (bins * places % (4 * seq)) * (np.pi / (2 * seq))
    return np.concatenate([np.cos(angles), np.sin(angles)]).astype(ml_dtypes.bfloat16)


def rows(count, width, dtype=jnp.bfloat16):
    return jax.ShapeDtypeStruct((count, width), dtype)


def call(body, outs, args, flops, scratch=(), limit=8192 * KIB, space=pltpu.VMEM):
    size = sum(a.size * a.dtype.itemsize for a in (*outs, *args))
    return pl.pallas_call(
        body,
        out_shape=outs,
        in_specs=[pl.BlockSpec(memory_space=space)] * len(args),
        out_specs=[pl.BlockSpec(memory_space=pltpu.VMEM)] * len(outs),
        scratch_shapes=list(scratch),
        compiler_params=pltpu.CompilerParams(vmem_limit_bytes=limit),
        cost_estimate=pl.CostEstimate(flops=flops, bytes_accessed=size, transcendentals=0),
    )(*args)


def part(index, size):
    return pl.ds(pl.multiple_of(index * size, size), size)


def behind(own, shift, parts):
    return lax.rem(own - shift + parts, parts)


def ahead(own, shift, parts):
    return lax.rem(own + shift, parts)


def split_body(parts, *refs):
    sources, pieces, (held, sems) = refs[:4], refs[4:-2], refs[-2:]
    copies = [pltpu.make_async_copy(source, held.at[n], sems.at[n]) for n, source in enumerate(sources)]
    for copy in copies:
        copy.start()
    outer, gate, inputs, taps = (held.at[n] for n in range(4))
    own = lax.axis_index("ctx")
    width = outer.shape[1] // parts
    for copy in copies:
        copy.wait()
    for shift in range(parts):
        lanes = part(ahead(own, shift, parts), width)
        pieces[shift][...] = taps[:, lanes]
        product = outer[:, lanes].astype(jnp.float32) * gate[:, lanes].astype(jnp.float32)
        pieces[parts + shift][...] = product.astype(jnp.bfloat16)
        pieces[2 * parts + shift][...] = inputs[:, lanes]


def load_body(table, gain, anchor, table_out, gain_out, sems):
    size = table.shape[0] // CHUNKS
    copies = [(table.at[pl.ds(n * size, size)], table_out.at[pl.ds(n * size, size)]) for n in range(CHUNKS)]
    copies = [pltpu.make_async_copy(*ends, sems.at[n]) for n, ends in enumerate(copies + [(gain, gain_out)])]
    for copy in copies:
        copy.start()
    for copy in copies:
        copy.wait()


def dot(first, second):
    return jnp.dot(first, second, preferred_element_type=jnp.float32)


def stack(pieces, out):
    own, parts, span = lax.axis_index("ctx"), len(pieces), pieces[0].shape[0]
    for shift, piece in enumerate(pieces):
        out[part(behind(own, shift, parts), span), :] = piece[...]


def correlate(first, second, table, both):
    seq = both.shape[0] // 2
    real, imag = first[:seq], first[seq:]
    cos, sin = second[:seq], second[seq:]
    both[:seq, :] = (real * cos + imag * sin).astype(jnp.bfloat16)
    both[seq:, :] = (imag * cos - real * sin).astype(jnp.bfloat16)
    product = lax.dot_general(table[...], both[...], (((0,), (0,)), ((), ())), preferred_element_type=jnp.float32)
    return product * (1.0 / seq)


def emit(outs, total):
    own, parts, span = lax.axis_index("ctx"), len(outs), outs[0].shape[0]
    for shift, out in enumerate(outs):
        out[...] = total[part(ahead(own, shift, parts), span), :].astype(jnp.bfloat16)


def input_body(parts, gain, *refs):
    tap_pieces, grad_pieces, refs = refs[:parts], refs[parts : 2 * parts], refs[2 * parts :]
    table, spec, refs = refs[0], refs[1], refs[2:]
    outs, (taps, grads, both, total) = refs[:parts], refs[parts:]
    stack(tap_pieces, taps)
    stack(grad_pieces, grads)
    grad_spec = dot(table[...], grads[...])
    spec[...] = grad_spec
    skip = gain[:, part(lax.axis_index("ctx"), taps.shape[1])] * grads[...].astype(jnp.float32)
    total[...] = correlate(grad_spec, dot(table[...], taps[...]), table, both) + skip
    emit(outs, total)


def filter_body(parts, spec, *refs):
    pieces, table, refs = refs[:parts], refs[parts], refs[parts + 1 :]
    outs, (inputs, both, total) = refs[:parts], refs[parts:]
    stack(pieces, inputs)
    total[...] = correlate(spec, dot(table[...], inputs[...]), table, both)
    emit(outs, total)


def join_body(*refs):
    pieces, out = refs[:-1], refs[-1]
    own, parts, width = lax.axis_index("ctx"), len(pieces), pieces[0].shape[1]
    for shift, piece in enumerate(pieces):
        out[:, part(behind(own, shift, parts), width)] = piece[...].astype(out.dtype)


def plain_shards(grad_out, gate_act, conv_input, filter_taps, skip_gain):
    span, channels = grad_out.shape
    parts = lax.axis_size("ctx")
    own = lax.axis_index("ctx")
    seq = span * parts
    width = channels // parts
    table = jnp.asarray(tables(seq))

    def swap(values, size, axis, place, other):
        pieces = [None] * parts
        for shift in range(parts):
            piece = lax.dynamic_slice_in_dim(values, (own + shift) % parts * size, size, axis)
            pairs = [(i, (i + shift) % parts) for i in range(parts)]
            pieces[-shift % parts] = lax.ppermute(piece, "ctx", pairs) if shift else piece
        ring = jnp.concatenate(pieces + pieces, axis=other)
        start = (parts - own) % parts * place
        return lax.dynamic_slice_in_dim(ring, start, parts * place, other)

    def correlate(first, second):
        real, imag = first[:seq], first[seq:]
        cos, sin = second[:seq], second[seq:]
        both = jnp.concatenate([real * cos + imag * sin, imag * cos - real * sin], axis=0).astype(jnp.bfloat16)
        return lax.dot_general(table, both, (((0,), (0,)), ((), ())), preferred_element_type=jnp.float32) * (1.0 / seq)

    grad_y = (grad_out.astype(jnp.float32) * gate_act.astype(jnp.float32)).astype(jnp.bfloat16)
    taps, grads, inputs = (swap(v, width, 1, span, 0) for v in (filter_taps, grad_y, conv_input))
    gain = lax.dynamic_slice_in_dim(skip_gain, own * width, width, 0)
    spec = dot(table, grads)
    grad_input = correlate(spec, dot(table, taps)) + gain[None, :] * grads.astype(jnp.float32)
    grad_filter = correlate(spec, dot(table, inputs))
    grad_input, grad_filter = (swap(v.astype(jnp.bfloat16), span, 0, width, 1) for v in (grad_input, grad_filter))
    return grad_input, grad_filter.astype(jnp.float32)


def shards(grad_out, gate_act, conv_input, filter_taps, skip_gain):
    span, channels = grad_out.shape
    parts = lax.axis_size("ctx")
    seq = span * parts
    width = channels // parts
    if width % 128 or span % 16 or parts != 4:
        return plain_shards(grad_out, gate_act, conv_input, filter_taps, skip_gain)

    def moved(pieces, shifts=ORDER):
        pieces = list(pieces)
        for shift in shifts:
            pieces[shift] = lax.ppermute(pieces[shift], "ctx", [(i, (i + shift) % parts) for i in range(parts)])
        return pieces

    small, bf16, f32 = rows(span, width), jnp.bfloat16, jnp.float32
    split = call(
        functools.partial(split_body, parts),
        [small] * (3 * parts),
        (grad_out, gate_act, conv_input, filter_taps),
        span * channels,
        (pltpu.VMEM((4, span, channels), bf16), pltpu.SemaphoreType.DMA((4,))),
        limit=54336 * KIB,
        space=pltpu.HBM,
    )
    taps = moved(split[:parts])
    grads = moved(split[parts : 2 * parts])
    inputs = list(split[2 * parts : 3 * parts])

    inputs = moved(inputs, ORDER)
    table, gain = call(
        load_body,
        [rows(2 * seq, seq), rows(1, channels, f32)],
        (jnp.asarray(tables(seq)), skip_gain[None, :], taps[ORDER[0]]),
        0,
        (pltpu.SemaphoreType.DMA((CHUNKS + 1,)),),
        limit=53312 * KIB,
        space=pltpu.HBM,
    )
    series, spectra, total = pltpu.VMEM((seq, width), bf16), pltpu.VMEM((2 * seq, width), bf16), pltpu.VMEM((seq, width), f32)
    spec, *grad_inputs = call(
        functools.partial(input_body, parts),
        [rows(2 * seq, width, f32)] + [small] * parts,
        (gain, *taps, *grads, table),
        12 * seq * seq * width,
        (series, series, spectra, total),
    )

    grad_inputs = moved(grad_inputs)
    grad_filters = call(
        functools.partial(filter_body, parts),
        [small] * parts,
        (spec, *inputs, table),
        8 * seq * seq * width,
        (series, spectra, total),
    )
    grad_filters = moved(grad_filters)
    grad_input = call(join_body, [rows(span, channels)], grad_inputs, 0)[0]
    grad_filter = call(join_body, [rows(span, channels, f32)], grad_filters, 0)[0]
    return grad_input, grad_filter


def solution(mesh):
    return jax.shard_map(
        shards,
        mesh=mesh,
        in_specs=(
            P(("grp", "ctx"), "chan"),
            P(("grp", "ctx"), "chan"),
            P(("grp", "ctx"), "chan"),
            P("ctx", "chan"),
            P("chan"),
        ),
        out_specs=(P(("grp", "ctx"), "chan"), P(("grp", "ctx"), "chan")),
        check_vma=False,
    )
```

time: 40.4 us -> 36.2 us (0.90)
  Pallas kernels: 0 us -> 7.38 us
  local copies, waits for them, and re-layouts: 6.71 us -> 0.01 us
  matrix products: 2.81 us -> 0 us
  waiting for transfers between devices: 5.4 us -> 2.99 us
  starting transfers between devices: 24 us -> 25 us
    pallas_call x0 -> x6, Pallas kernels: none -> 7.38 us  [call(): pl.pallas_call(body, out_shape=outs, in_specs=[pl.BlockSpec(memory_space=...]
    unnamed x47 -> x2, local copies, waits for them, and re-layouts: 4.68 us -> 0.01 us
    dot_general x7 -> x0, matrix products: 2.81 us -> none  [the longest x4 1.45 us: correlate(): return jnp.dot(inverse, both, preferred_element_type=jnp.float32)]
    ppermute x15, waiting for transfers between devices: 5.4 us -> 2.99 us  [moved(): lax.ppermute(pieces[shift], 'ctx', [(i, (i + shift) % parts) for i in ran...]
    dynamic_slice x7 -> x0, local copies, waits for them, and re-layouts: 1.97 us -> none  [the longest x3 1.08 us: scatter(): lax.dynamic_slice_in_dim(values, target * width, width, 1)]
    ppermute x15, starting transfers between devices: 24 us -> 25 us  [moved(): lax.ppermute(pieces[shift], 'ctx', [(i, (i + shift) % parts) for i in ran...]
  transfers between devices with their start and end apart: 15 -> 15, of which waited for: 6 -> 2; matrix products, arithmetic and copies ran while one was open for 16% -> 0% of each run, Pallas kernels for 0% -> 14%
where the time goes in v2:
time: 36.2 us; the launch traced here: 36.1 us
  starting transfers between devices  25 us (69%)
  Pallas kernels  7.38 us (20%)
  waiting for transfers between devices  2.99 us (8%)
  between operations  0.69 us (2%)
    ppermute x15, starting transfers between devices, moved(): lax.ppermute(pieces[shift], 'ctx', [(i, (i + shift) % parts) for i in ran...  25 us
    pallas_call x6, Pallas kernels, call(): pl.pallas_call(body, out_shape=outs, in_specs=[pl.BlockSpec(memory_space=...  7.38 us
    ppermute x15, waiting for transfers between devices, moved(): lax.ppermute(pieces[shift], 'ctx', [(i, (i + shift) % parts) for i in ran...  2.99 us
  transfers between devices with their start and end apart: 15, of which 2 were waited for; matrix products, arithmetic and copies ran while one was open for 0% of the time, Pallas kernels for 14%

profile of v2, /device:TPU:0, one launch (start us, length us, event | category | flops | bytes accessed | tf_op | source)
XLA Modules:
  0.0 36.1 jit_solution(310571306334897947)
XLA Ops:
  0.6 1.4 %shard_map.77 = (bf16[128,256]{1,0:T(8,128)(2,1)S(1)}, bf16[128,256]{1,0:T(8,128)(2,1)S(1)}, bf16[128,256]{1,0:T(8,128)(2,1)S(1)}, bf16[128,256]{1,0:T(8,128)(2,...) custom-call(bf16[128,1024]{1,0:T(8,128)(2,1)} %refs_0_.1, ...), custom_call_target="tpu_custom_call" | custom-call | flops 131072 | bytes 1835008 | tf_op jit(solution)/shard_map/pallas_call | solution.py:31
  2.0 3.1 %collective-permute-start = (bf16[128,256]{1,0:T(8,128)(2,1)S(1)}, bf16[128,256]{1,0:T(8,128)(2,1)S(1)}, u32[]{:S(2)}, u32[]{:S(2)}) collective-permute-start(bf16[128,256]{1,0:T(8,128)(2,1)S(1)} %get-tuple-element.25), channel_id=1, source_target_pairs={{0,4},{4,8},{8,12},{12,0},{1,5},{5,9},{9,13},{13,1},{2,6},{6,10},{... | collective-permute-start | bytes 196616 | tf_op jit(solution)/shard_map/ppermute | solution.py:181
  5.1 2.6 %collective-permute-start.1 = (bf16[128,256]{1,0:T(8,128)(2,1)S(1)}, bf16[128,256]{1,0:T(8,128)(2,1)S(1)}, u32[]{:S(2)}, u32[]{:S(2)}) collective-permute-start(bf16[128,256]{1,0:T(8,128)(2,1)S(1)} %get-tuple-element.28), channel_id=1, source_target_pairs={{0,8},{4,12},{8,0},{12,4},{1,9},{5,13},{9,1},{13,5},{2,10},{6,14},... | collective-permute-start | bytes 196616 | tf_op jit(solution)/shard_map/ppermute | solution.py:181
  7.7 1.3 %collective-permute-start.2 = (bf16[128,256]{1,0:T(8,128)(2,1)S(1)}, bf16[128,256]{1,0:T(8,128)(2,1)S(1)}, u32[]{:S(2)}, u32[]{:S(2)}) collective-permute-start(bf16[128,256]{1,0:T(8,128)(2,1)S(1)} %get-tuple-element.29), channel_id=1, source_target_pairs={{0,12},{4,0},{8,4},{12,8},{1,13},{5,1},{9,5},{13,9},{2,14},{6,2},{... | collective-permute-start | bytes 196616 | tf_op jit(solution)/shard_map/ppermute | solution.py:181
  9.0 0.7 %collective-permute-start.3 = (bf16[128,256]{1,0:T(8,128)(2,1)S(1)}, bf16[128,256]{1,0:T(8,128)(2,1)S(1)}, u32[]{:S(2)}, u32[]{:S(2)}) collective-permute-start(bf16[128,256]{1,0:T(8,128)(2,1)S(1)} %get-tuple-element.31), channel_id=1, source_target_pairs={{0,4},{4,8},{8,12},{12,0},{1,5},{5,9},{9,13},{13,1},{2,6},{6,10},{... | collective-permute-start | bytes 196616 | tf_op jit(solution)/shard_map/ppermute | solution.py:181
  9.7 0.3 collective-permute-start.4
  10.0 0.0 collective-permute-done.anchor.refs_1_
  10.0 2.8 %collective-permute-start.5 = (bf16[128,256]{1,0:T(8,128)(2,1)S(1)}, bf16[128,256]{1,0:T(8,128)(2,1)S(1)}, u32[]{:S(2)}, u32[]{:S(2)}) collective-permute-start(bf16[128,256]{1,0:T(8,128)(2,1)S(1)} %get-tuple-element.33), channel_id=1, source_target_pairs={{0,12},{4,0},{8,4},{12,8},{1,13},{5,1},{9,5},{13,9},{2,14},{6,2},{... | collective-permute-start | bytes 196616 | tf_op jit(solution)/shard_map/ppermute | solution.py:181
  12.9 1.4 %shard_map.78 = (bf16[1024,512]{1,0:T(8,128)(2,1)S(1)}, f32[1,1024]{1,0:T(1,128)S(1)}) custom-call(bf16[1024,512]{1,0:T(8,128)(2,1)} %constant.2.clone.table, f32[1,1024]{1,0:T(1,128)S(1)} %bitcast.1, bf16[128,256]{1,0:T(8,128)(2,1)S(1)} %collective-permute-done.anchor.refs_1_), custom_call_target="tpu_custom_call" | custom-call | bytes 2170880 | tf_op jit(solution)/shard_map/pallas_call | solution.py:31
  14.2 0.0 collective-permute-done.1.refs_2_
  14.2 0.6 %collective-permute-start.9 = (bf16[128,256]{1,0:T(8,128)(2,1)S(1)}, bf16[128,256]{1,0:T(8,128)(2,1)S(1)}, u32[]{:S(2)}, u32[]{:S(2)}) collective-permute-start(bf16[128,256]{1,0:T(8,128)(2,1)S(1)} %get-tuple-element.41), channel_id=1, source_target_pairs={{0,4},{4,8},{8,12},{12,0},{1,5},{5,9},{9,13},{13,1},{2,6},{6,10},{... | collective-permute-start | bytes 196616 | tf_op jit(solution)/shard_map/ppermute | solution.py:181
  14.9 0.0 collective-permute-done.2.refs_3_
  14.9 2.9 %collective-permute-start.10 = (bf16[128,256]{1,0:T(8,128)(2,1)S(1)}, bf16[128,256]{1,0:T(8,128)(2,1)S(1)}, u32[]{:S(2)}, u32[]{:S(2)}) collective-permute-start(bf16[128,256]{1,0:T(8,128)(2,1)S(1)} %get-tuple-element.42), channel_id=1, source_target_pairs={{0,8},{4,12},{8,0},{12,4},{1,9},{5,13},{9,1},{13,5},{2,10},{6,14},... | collective-permute-start | bytes 196616 | tf_op jit(solution)/shard_map/ppermute | solution.py:181
  17.8 0.0 collective-permute-done.3.refs_5_
  17.8 1.5 %collective-permute-start.11 = (bf16[128,256]{1,0:T(8,128)(2,1)S(1)}, bf16[128,256]{1,0:T(8,128)(2,1)S(1)}, u32[]{:S(2)}, u32[]{:S(2)}) collective-permute-start(bf16[128,256]{1,0:T(8,128)(2,1)S(1)} %get-tuple-element.43), channel_id=1, source_target_pairs={{0,12},{4,0},{8,4},{12,8},{1,13},{5,1},{9,5},{13,9},{2,14},{6,2},{... | collective-permute-start | bytes 196616 | tf_op jit(solution)/shard_map/ppermute | solution.py:181
  19.3 0.0 collective-permute-done.4.refs_6_
  19.3 0.0 collective-permute-done.5.refs_7_
  19.3 1.7 %shard_map.79 = (f32[1024,256]{1,0:T(8,128)S(1)}, bf16[128,256]{1,0:T(8,128)(2,1)S(1)}, bf16[128,256]{1,0:T(8,128)(2,1)S(1)}, bf16[128,256]{1,0:T(8,128)(2,1)S(1)}, bf16[128,256]{1,0:T(8,128)(2,1)S(1)}) custom-call(f32[1,1024]{1,0:T(1,128)S(1)} %get-tuple-element.26.gain, bf16[128,256]{1,0:T(8,128)(2,1)S(1)} %get-tuple-element.27.refs_0_, ...), custom_call_target="tpu_custom_call" | custom-call | flops 805306368 | bytes 2887680 | tf_op jit(solution)/shard_map/pallas_call | solution.py:31
  21.0 2.8 %collective-permute-start.6 = (bf16[128,256]{1,0:T(8,128)(2,1)S(1)}, bf16[128,256]{1,0:T(8,128)(2,1)S(1)}, u32[]{:S(2)}, u32[]{:S(2)}) collective-permute-start(bf16[128,256]{1,0:T(8,128)(2,1)S(1)} %get-tuple-element.36), channel_id=1, source_target_pairs={{0,4},{4,8},{8,12},{12,0},{1,5},{5,9},{9,13},{13,1},{2,6},{6,10},{... | collective-permute-start | bytes 196616 | tf_op jit(solution)/shard_map/ppermute | solution.py:181
  23.8 1.0 %collective-permute-start.7 = (bf16[128,256]{1,0:T(8,128)(2,1)S(1)}, bf16[128,256]{1,0:T(8,128)(2,1)S(1)}, u32[]{:S(2)}, u32[]{:S(2)}) collective-permute-start(bf16[128,256]{1,0:T(8,128)(2,1)S(1)} %get-tuple-element.37), channel_id=1, source_target_pairs={{0,8},{4,12},{8,0},{12,4},{1,9},{5,13},{9,1},{13,5},{2,10},{6,14},... | collective-permute-start | bytes 196616 | tf_op jit(solution)/shard_map/ppermute | solution.py:181
  24.8 1.4 %collective-permute-start.8 = (bf16[128,256]{1,0:T(8,128)(2,1)S(1)}, bf16[128,256]{1,0:T(8,128)(2,1)S(1)}, u32[]{:S(2)}, u32[]{:S(2)}) collective-permute-start(bf16[128,256]{1,0:T(8,128)(2,1)S(1)} %get-tuple-element.38), channel_id=1, source_target_pairs={{0,12},{4,0},{8,4},{12,8},{1,13},{5,1},{9,5},{13,9},{2,14},{6,2},{... | collective-permute-start | bytes 196616 | tf_op jit(solution)/shard_map/ppermute | solution.py:181
  26.2 0.0 collective-permute-done.11.refs_3_
  26.2 1.4 %shard_map.81 = (bf16[128,256]{1,0:T(8,128)(2,1)S(1)}, bf16[128,256]{1,0:T(8,128)(2,1)S(1)}, bf16[128,256]{1,0:T(8,128)(2,1)S(1)}, bf16[128,256]{1,0:T(8,128)(2,1)S(1)}) custom-call(f32[1024,256]{1,0:T(8,128)S(1)} %get-tuple-element.39.spec, bf16[128,256]{1,0:T(8,128)(2,1)S(1)} %get-tuple-element.40.refs_0_, ...), custom_call_target="tpu_custom_call" | custom-call | flops 536870912 | bytes 2621440 | tf_op jit(solution)/shard_map/pallas_call | solution.py:31
  27.6 0.7 %collective-permute-start.12 = (bf16[128,256]{1,0:T(8,128)(2,1)S(1)}, bf16[128,256]{1,0:T(8,128)(2,1)S(1)}, u32[]{:S(2)}, u32[]{:S(2)}) collective-permute-start(bf16[128,256]{1,0:T(8,128)(2,1)S(1)} %get-tuple-element.45), channel_id=1, source_target_pairs={{0,4},{4,8},{8,12},{12,0},{1,5},{5,9},{9,13},{13,1},{2,6},{6,10},{... | collective-permute-start | bytes 196616 | tf_op jit(solution)/shard_map/ppermute | solution.py:181
  28.3 1.9 %collective-permute-start.13 = (bf16[128,256]{1,0:T(8,128)(2,1)S(1)}, bf16[128,256]{1,0:T(8,128)(2,1)S(1)}, u32[]{:S(2)}, u32[]{:S(2)}) collective-permute-start(bf16[128,256]{1,0:T(8,128)(2,1)S(1)} %get-tuple-element.46), channel_id=1, source_target_pairs={{0,8},{4,12},{8,0},{12,4},{1,9},{5,13},{9,1},{13,5},{2,10},{6,14},... | collective-permute-start | bytes 196616 | tf_op jit(solution)/shard_map/ppermute | solution.py:181
  30.2 0.0 collective-permute-done.6.refs_1_
  30.2 1.3 %collective-permute-start.14 = (bf16[128,256]{1,0:T(8,128)(2,1)S(1)}, bf16[128,256]{1,0:T(8,128)(2,1)S(1)}, u32[]{:S(2)}, u32[]{:S(2)}) collective-permute-start(bf16[128,256]{1,0:T(8,128)(2,1)S(1)} %get-tuple-element.47), channel_id=1, source_target_pairs={{0,12},{4,0},{8,4},{12,8},{1,13},{5,1},{9,5},{13,9},{2,14},{6,2},{... | collective-permute-start | bytes 196616 | tf_op jit(solution)/shard_map/ppermute | solution.py:181
  31.5 0.7 %shard_map.80 = bf16[128,1024]{1,0:T(8,128)(2,1)} custom-call(bf16[128,256]{1,0:T(8,128)(2,1)S(1)} %get-tuple-element.35.refs_0_, bf16[128,256]{1,0:T(8,128)(2,1)S(1)} %collective-permute-done.6.refs_1_, bf16[128,256]{1,0:T(8,128)(2,1)S(1)} %collective-permute-done.7.refs_2_, bf16[128,256]{1,0:T(8,128)(2,1)S(1)} %collective-permute-done.8.refs_3_), custom_call_target="tpu_custom_call" | custom-call | bytes 524288 | tf_op jit(solution)/shard_map/pallas_call | solution.py:31
  32.3 1.6 %collective-permute-done.12.refs_1_ = bf16[128,256]{1,0:T(8,128)(2,1)S(1)} collective-permute-done((bf16[128,256]{1,0:T(8,128)(2,1)S(1)}, bf16[128,256]{1,0:T(8,128)(2,1)S(1)}, u32[]{:S(2)}, u32[]{:S(2)}) %collective-permute-start.12) | collective-permute-done | bytes 65568 | tf_op jit(solution)/shard_map/ppermute | solution.py:181
  33.9 1.4 %collective-permute-done.13.refs_2_ = bf16[128,256]{1,0:T(8,128)(2,1)S(1)} collective-permute-done((bf16[128,256]{1,0:T(8,128)(2,1)S(1)}, bf16[128,256]{1,0:T(8,128)(2,1)S(1)}, u32[]{:S(2)}, u32[]{:S(2)}) %collective-permute-start.13) | collective-permute-done | bytes 65568 | tf_op jit(solution)/shard_map/ppermute | solution.py:181
  35.2 0.0 collective-permute-done.14.refs_3_
  35.2 0.8 %shard_map.82 = f32[128,1024]{1,0:T(8,128)} custom-call(bf16[128,256]{1,0:T(8,128)(2,1)S(1)} %get-tuple-element.44.refs_0_, bf16[128,256]{1,0:T(8,128)(2,1)S(1)} %collective-permute-done.12.refs_1_, bf16[128,256]{1,0:T(8,128)(2,1)S(1)} %collective-permute-done.13.refs_2_, bf16[128,256]{1,0:T(8,128)(2,1)S(1)} %collective-permute-done.14.refs_3_), custom_call_target="tpu_custom_call" | custom-call | bytes 786432 | tf_op jit(solution)/shard_map/pallas_call | solution.py:31
  (6 shorter events, 0.0 us)
Async XLA Ops:
  2.0 8.0 %collective-permute-start = (bf16[128,256]{1,0:T(8,128)(2,1)S(1)}, bf16[128,256]{1,0:T(8,128)(2,1)S(1)}, u32[]{:S(2)}, u32[]{:S(2)}) collective-permute-start(bf16[128,256]{1,0:T(8,128)(2,1)S(1)} %get-tuple-element.25), channel_id=1, source_target_pairs={{0,4},{4,8},{8,12},{12,0},{1,5},{5,9},{9,13},{13,1},{2,6},{6,10},{... | collective-permute-start | bytes 196616 | tf_op jit(solution)/shard_map/ppermute | solution.py:181
  5.1 9.1 %collective-permute-start.1 = (bf16[128,256]{1,0:T(8,128)(2,1)S(1)}, bf16[128,256]{1,0:T(8,128)(2,1)S(1)}, u32[]{:S(2)}, u32[]{:S(2)}) collective-permute-start(bf16[128,256]{1,0:T(8,128)(2,1)S(1)} %get-tuple-element.28), channel_id=1, source_target_pairs={{0,8},{4,12},{8,0},{12,4},{1,9},{5,13},{9,1},{13,5},{2,10},{6,14},... | collective-permute-start | bytes 196616 | tf_op jit(solution)/shard_map/ppermute | solution.py:181
  7.7 5.2 %copy-start = (f32[1024]{0:T(1024)S(1)}, f32[1024]{0:T(1024)}, u32[]{:S(2)}) copy-start(f32[1024]{0:T(1024)} %param.10) | copy-start | bytes 12292
  7.7 7.2 %collective-permute-start.2 = (bf16[128,256]{1,0:T(8,128)(2,1)S(1)}, bf16[128,256]{1,0:T(8,128)(2,1)S(1)}, u32[]{:S(2)}, u32[]{:S(2)}) collective-permute-start(bf16[128,256]{1,0:T(8,128)(2,1)S(1)} %get-tuple-element.29), channel_id=1, source_target_pairs={{0,12},{4,0},{8,4},{12,8},{1,13},{5,1},{9,5},{13,9},{2,14},{6,2},{... | collective-permute-start | bytes 196616 | tf_op jit(solution)/shard_map/ppermute | solution.py:181
  9.0 8.8 %collective-permute-start.3 = (bf16[128,256]{1,0:T(8,128)(2,1)S(1)}, bf16[128,256]{1,0:T(8,128)(2,1)S(1)}, u32[]{:S(2)}, u32[]{:S(2)}) collective-permute-start(bf16[128,256]{1,0:T(8,128)(2,1)S(1)} %get-tuple-element.31), channel_id=1, source_target_pairs={{0,4},{4,8},{8,12},{12,0},{1,5},{5,9},{9,13},{13,1},{2,6},{6,10},{... | collective-permute-start | bytes 196616 | tf_op jit(solution)/shard_map/ppermute | solution.py:181
  9.7 9.6 %collective-permute-start.4 = (bf16[128,256]{1,0:T(8,128)(2,1)S(1)}, bf16[128,256]{1,0:T(8,128)(2,1)S(1)}, u32[]{:S(2)}, u32[]{:S(2)}) collective-permute-start(bf16[128,256]{1,0:T(8,128)(2,1)S(1)} %get-tuple-element.32), channel_id=1, source_target_pairs={{0,8},{4,12},{8,0},{12,4},{1,9},{5,13},{9,1},{13,5},{2,10},{6,14},... | collective-permute-start | bytes 196616 | tf_op jit(solution)/shard_map/ppermute | solution.py:181
  10.0 9.3 %collective-permute-start.5 = (bf16[128,256]{1,0:T(8,128)(2,1)S(1)}, bf16[128,256]{1,0:T(8,128)(2,1)S(1)}, u32[]{:S(2)}, u32[]{:S(2)}) collective-permute-start(bf16[128,256]{1,0:T(8,128)(2,1)S(1)} %get-tuple-element.33), channel_id=1, source_target_pairs={{0,12},{4,0},{8,4},{12,8},{1,13},{5,1},{9,5},{13,9},{2,14},{6,2},{... | collective-permute-start | bytes 196616 | tf_op jit(solution)/shard_map/ppermute | solution.py:181
  14.2 10.6 %collective-permute-start.9 = (bf16[128,256]{1,0:T(8,128)(2,1)S(1)}, bf16[128,256]{1,0:T(8,128)(2,1)S(1)}, u32[]{:S(2)}, u32[]{:S(2)}) collective-permute-start(bf16[128,256]{1,0:T(8,128)(2,1)S(1)} %get-tuple-element.41), channel_id=1, source_target_pairs={{0,4},{4,8},{8,12},{12,0},{1,5},{5,9},{9,13},{13,1},{2,6},{6,10},{... | collective-permute-start | bytes 196616 | tf_op jit(solution)/shard_map/ppermute | solution.py:181
  14.9 11.4 %collective-permute-start.10 = (bf16[128,256]{1,0:T(8,128)(2,1)S(1)}, bf16[128,256]{1,0:T(8,128)(2,1)S(1)}, u32[]{:S(2)}, u32[]{:S(2)}) collective-permute-start(bf16[128,256]{1,0:T(8,128)(2,1)S(1)} %get-tuple-element.42), channel_id=1, source_target_pairs={{0,8},{4,12},{8,0},{12,4},{1,9},{5,13},{9,1},{13,5},{2,10},{6,14},... | collective-permute-start | bytes 196616 | tf_op jit(solution)/shard_map/ppermute | solution.py:181
  17.8 8.4 %collective-permute-start.11 = (bf16[128,256]{1,0:T(8,128)(2,1)S(1)}, bf16[128,256]{1,0:T(8,128)(2,1)S(1)}, u32[]{:S(2)}, u32[]{:S(2)}) collective-permute-start(bf16[128,256]{1,0:T(8,128)(2,1)S(1)} %get-tuple-element.43), channel_id=1, source_target_pairs={{0,12},{4,0},{8,4},{12,8},{1,13},{5,1},{9,5},{13,9},{2,14},{6,2},{... | collective-permute-start | bytes 196616 | tf_op jit(solution)/shard_map/ppermute | solution.py:181
  21.0 9.2 %collective-permute-start.6 = (bf16[128,256]{1,0:T(8,128)(2,1)S(1)}, bf16[128,256]{1,0:T(8,128)(2,1)S(1)}, u32[]{:S(2)}, u32[]{:S(2)}) collective-permute-start(bf16[128,256]{1,0:T(8,128)(2,1)S(1)} %get-tuple-element.36), channel_id=1, source_target_pairs={{0,4},{4,8},{8,12},{12,0},{1,5},{5,9},{9,13},{13,1},{2,6},{6,10},{... | collective-permute-start | bytes 196616 | tf_op jit(solution)/shard_map/ppermute | solution.py:181
  23.8 7.7 %collective-permute-start.7 = (bf16[128,256]{1,0:T(8,128)(2,1)S(1)}, bf16[128,256]{1,0:T(8,128)(2,1)S(1)}, u32[]{:S(2)}, u32[]{:S(2)}) collective-permute-start(bf16[128,256]{1,0:T(8,128)(2,1)S(1)} %get-tuple-element.37), channel_id=1, source_target_pairs={{0,8},{4,12},{8,0},{12,4},{1,9},{5,13},{9,1},{13,5},{2,10},{6,14},... | collective-permute-start | bytes 196616 | tf_op jit(solution)/shard_map/ppermute | solution.py:181
  24.8 6.7 %collective-permute-start.8 = (bf16[128,256]{1,0:T(8,128)(2,1)S(1)}, bf16[128,256]{1,0:T(8,128)(2,1)S(1)}, u32[]{:S(2)}, u32[]{:S(2)}) collective-permute-start(bf16[128,256]{1,0:T(8,128)(2,1)S(1)} %get-tuple-element.38), channel_id=1, source_target_pairs={{0,12},{4,0},{8,4},{12,8},{1,13},{5,1},{9,5},{13,9},{2,14},{6,2},{... | collective-permute-start | bytes 196616 | tf_op jit(solution)/shard_map/ppermute | solution.py:181
  27.6 6.2 %collective-permute-start.12 = (bf16[128,256]{1,0:T(8,128)(2,1)S(1)}, bf16[128,256]{1,0:T(8,128)(2,1)S(1)}, u32[]{:S(2)}, u32[]{:S(2)}) collective-permute-start(bf16[128,256]{1,0:T(8,128)(2,1)S(1)} %get-tuple-element.45), channel_id=1, source_target_pairs={{0,4},{4,8},{8,12},{12,0},{1,5},{5,9},{9,13},{13,1},{2,6},{6,10},{... | collective-permute-start | bytes 196616 | tf_op jit(solution)/shard_map/ppermute | solution.py:181
  28.3 6.9 %collective-permute-start.13 = (bf16[128,256]{1,0:T(8,128)(2,1)S(1)}, bf16[128,256]{1,0:T(8,128)(2,1)S(1)}, u32[]{:S(2)}, u32[]{:S(2)}) collective-permute-start(bf16[128,256]{1,0:T(8,128)(2,1)S(1)} %get-tuple-element.46), channel_id=1, source_target_pairs={{0,8},{4,12},{8,0},{12,4},{1,9},{5,13},{9,1},{13,5},{2,10},{6,14},... | collective-permute-start | bytes 196616 | tf_op jit(solution)/shard_map/ppermute | solution.py:181
  30.2 5.0 %collective-permute-start.14 = (bf16[128,256]{1,0:T(8,128)(2,1)S(1)}, bf16[128,256]{1,0:T(8,128)(2,1)S(1)}, u32[]{:S(2)}, u32[]{:S(2)}) collective-permute-start(bf16[128,256]{1,0:T(8,128)(2,1)S(1)} %get-tuple-element.47), channel_id=1, source_target_pairs={{0,12},{4,0},{8,4},{12,8},{1,13},{5,1},{9,5},{13,9},{2,14},{6,2},{... | collective-permute-start | bytes 196616 | tf_op jit(solution)/shard_map/ppermute | solution.py:181

commit v3 on v2

--- a/solution.py
+++ b/solution.py
@@ -11,7 +11,8 @@
 
 KIB = 1 << 10
 CHUNKS = 8
-ORDER = (1, 2, 3)
+PIECES = 2
+H, G, U, I, F = ((0,2,3,1),(0,1,2,3),(0,1,2,3),(0,1,2,3),(0,1,2,3))
 
 
 @functools.cache
@@ -83,20 +84,29 @@
     return jnp.dot(first, second, preferred_element_type=jnp.float32)
 
 
-def stack(pieces, out):
+def stack(pieces, out, order):
     own, parts, span = lax.axis_index("ctx"), len(pieces), pieces[0].shape[0]
-    for shift, piece in enumerate(pieces):
+    for shift, piece in zip(order, pieces):
         out[part(behind(own, shift, parts), span), :] = piece[...]
 
 
-def correlate(first, second, table, both):
-    seq = both.shape[0] // 2
-    real, imag = first[:seq], first[seq:]
-    cos, sin = second[:seq], second[seq:]
-    both[:seq, :] = (real * cos + imag * sin).astype(jnp.bfloat16)
-    both[seq:, :] = (imag * cos - real * sin).astype(jnp.bfloat16)
-    product = lax.dot_general(table[...], both[...], (((0,), (0,)), ((), ())), preferred_element_type=jnp.float32)
-    return product * (1.0 / seq)
+def correlate(grads, seconds, table, spec, fresh):
+    seq = grads.shape[0] if fresh else seconds.shape[0]
+    size = seq // PIECES
+    total = None
+    for n in range(PIECES):
+        cos_rows, sin_rows = slice(n * size, (n + 1) * size), slice(seq + n * size, seq + (n + 1) * size)
+        if fresh:
+            real, imag = dot(table[cos_rows, :], grads[...]), dot(table[sin_rows, :], grads[...])
+            spec[cos_rows, :], spec[sin_rows, :] = real, imag
+        else:
+            real, imag = spec[cos_rows, :], spec[sin_rows, :]
+        cos, sin = dot(table[cos_rows, :], seconds[...]), dot(table[sin_rows, :], seconds[...])
+        both = (real * cos + imag * sin).astype(jnp.bfloat16), (imag * cos - real * sin).astype(jnp.bfloat16)
+        for rows_at, values in zip((cos_rows, sin_rows), both):
+            term = lax.dot_general(table[rows_at, :], values, (((0,), (0,)), ((), ())), preferred_element_type=jnp.float32)
+            total = term if total is None else total + term
+    return total * (1.0 / seq)
 
 
 def emit(outs, total):
@@ -109,27 +119,25 @@
     tap_pieces, grad_pieces, refs = refs[:parts], refs[parts : 2 * parts], refs[2 * parts :]
     table, spec, refs = refs[0], refs[1], refs[2:]
     outs, (taps, grads, both, total) = refs[:parts], refs[parts:]
-    stack(tap_pieces, taps)
-    stack(grad_pieces, grads)
-    grad_spec = dot(table[...], grads[...])
-    spec[...] = grad_spec
+    stack(tap_pieces, taps, H)
+    stack(grad_pieces, grads, G)
     skip = gain[:, part(lax.axis_index("ctx"), taps.shape[1])] * grads[...].astype(jnp.float32)
-    total[...] = correlate(grad_spec, dot(table[...], taps[...]), table, both) + skip
+    total[...] = correlate(grads, taps, table, spec, True) + skip
     emit(outs, total)
 
 
 def filter_body(parts, spec, *refs):
     pieces, table, refs = refs[:parts], refs[parts], refs[parts + 1 :]
     outs, (inputs, both, total) = refs[:parts], refs[parts:]
-    stack(pieces, inputs)
-    total[...] = correlate(spec, dot(table[...], inputs[...]), table, both)
+    stack(pieces, inputs, U)
+    total[...] = correlate(None, inputs, table, spec, False)
     emit(outs, total)
 
 
-def join_body(*refs):
+def join_body(order, *refs):
     pieces, out = refs[:-1], refs[-1]
     own, parts, width = lax.axis_index("ctx"), len(pieces), pieces[0].shape[1]
-    for shift, piece in enumerate(pieces):
+    for shift, piece in zip(order, pieces):
         out[:, part(behind(own, shift, parts), width)] = piece[...].astype(out.dtype)
 
 
@@ -175,11 +183,9 @@
     if width % 128 or span % 16 or parts != 4:
         return plain_shards(grad_out, gate_act, conv_input, filter_taps, skip_gain)
 
-    def moved(pieces, shifts=ORDER):
-        pieces = list(pieces)
-        for shift in shifts:
-            pieces[shift] = lax.ppermute(pieces[shift], "ctx", [(i, (i + shift) % parts) for i in range(parts)])
-        return pieces
+    def moved(pieces, order):
+        pairs = [[(i, (i + shift) % parts) for i in range(parts)] for shift in order]
+        return [lax.ppermute(pieces[n], "ctx", pair) if n else pieces[n] for n, pair in zip(order, pairs)]
 
     small, bf16, f32 = rows(span, width), jnp.bfloat16, jnp.float32
     split = call(
@@ -191,15 +197,13 @@
         limit=54336 * KIB,
         space=pltpu.HBM,
     )
-    taps = moved(split[:parts])
-    grads = moved(split[parts : 2 * parts])
-    inputs = list(split[2 * parts : 3 * parts])
-
-    inputs = moved(inputs, ORDER)
+    taps = moved(split[:parts], H)
+    grads = moved(split[parts : 2 * parts], G)
+    inputs = moved(split[2 * parts :], U)
     table, gain = call(
         load_body,
         [rows(2 * seq, seq), rows(1, channels, f32)],
-        (jnp.asarray(tables(seq)), skip_gain[None, :], taps[ORDER[0]]),
+        (jnp.asarray(tables(seq)), skip_gain[None, :], taps[1]),
         0,
         (pltpu.SemaphoreType.DMA((CHUNKS + 1,)),),
         limit=53312 * KIB,
@@ -213,8 +217,7 @@
         12 * seq * seq * width,
         (series, series, spectra, total),
     )
-
-    grad_inputs = moved(grad_inputs)
+    grad_inputs = moved(grad_inputs, I)
     grad_filters = call(
         functools.partial(filter_body, parts),
         [small] * parts,
@@ -222,9 +225,9 @@
         8 * seq * seq * width,
         (series, spectra, total),
     )
-    grad_filters = moved(grad_filters)
-    grad_input = call(join_body, [rows(span, channels)], grad_inputs, 0)[0]
-    grad_filter = call(join_body, [rows(span, channels, f32)], grad_filters, 0)[0]
+    grad_filters = moved(grad_filters, F)
+    grad_input = call(functools.partial(join_body, I), [rows(span, channels)], grad_inputs, 0)[0]
+    grad_filter = call(functools.partial(join_body, F), [rows(span, channels, f32)], grad_filters, 0)[0]
     return grad_input, grad_filter
 
 

time: 36.2 us -> 36.1 us (level)
  waiting for transfers between devices: 2.99 us -> 2.28 us
  starting transfers between devices: 25 us -> 25.7 us
    ppermute x15, starting transfers between devices: 25 us -> 25.7 us  [moved(): lax.ppermute(pieces[n], 'ctx', pair)]
    ppermute x15, waiting for transfers between devices: 2.99 us -> 2.28 us  [moved(): lax.ppermute(pieces[n], 'ctx', pair)]
where the time goes in v3:
time: 36.1 us; the launch traced here: 36 us
  starting transfers between devices  25.7 us (71%)
  Pallas kernels  7.26 us (20%)
  waiting for transfers between devices  2.28 us (6%)
  between operations  0.7 us (2%)
    ppermute x15, starting transfers between devices, moved(): lax.ppermute(pieces[n], 'ctx', pair)  25.7 us
    pallas_call x6, Pallas kernels, call(): pl.pallas_call(body, out_shape=outs, in_specs=[pl.BlockSpec(memory_space=...  7.26 us
    ppermute x15, waiting for transfers between devices, moved(): lax.ppermute(pieces[n], 'ctx', pair)  2.28 us
  transfers between devices with their start and end apart: 15, of which 2 were waited for; matrix products, arithmetic and copies ran while one was open for 0% of the time, Pallas kernels for 14%

profile of v3, /device:TPU:0, one launch (start us, length us, event | category | flops | bytes accessed | tf_op | source)
XLA Modules:
  0.0 36.0 jit_solution(1350375148827456041)
XLA Ops:
  0.6 1.4 %shard_map.77 = (bf16[128,256]{1,0:T(8,128)(2,1)S(1)}, bf16[128,256]{1,0:T(8,128)(2,1)S(1)}, bf16[128,256]{1,0:T(8,128)(2,1)S(1)}, bf16[128,256]{1,0:T(8,128)(2,...) custom-call(bf16[128,1024]{1,0:T(8,128)(2,1)} %refs_0_.1, ...), custom_call_target="tpu_custom_call" | custom-call | flops 131072 | bytes 1835008 | tf_op jit(solution)/shard_map/pallas_call | solution.py:32
  2.0 4.1 %collective-permute-start = (bf16[128,256]{1,0:T(8,128)(2,1)S(1)}, bf16[128,256]{1,0:T(8,128)(2,1)S(1)}, u32[]{:S(2)}, u32[]{:S(2)}) collective-permute-start(bf16[128,256]{1,0:T(8,128)(2,1)S(1)} %get-tuple-element.25), channel_id=1, source_target_pairs={{0,8},{4,12},{8,0},{12,4},{1,9},{5,13},{9,1},{13,5},{2,10},{6,14},... | collective-permute-start | bytes 196616 | tf_op jit(solution)/shard_map/ppermute | solution.py:188
  6.1 1.3 %collective-permute-start.1 = (bf16[128,256]{1,0:T(8,128)(2,1)S(1)}, bf16[128,256]{1,0:T(8,128)(2,1)S(1)}, u32[]{:S(2)}, u32[]{:S(2)}) collective-permute-start(bf16[128,256]{1,0:T(8,128)(2,1)S(1)} %get-tuple-element.28), channel_id=1, source_target_pairs={{0,12},{4,0},{8,4},{12,8},{1,13},{5,1},{9,5},{13,9},{2,14},{6,2},{... | collective-permute-start | bytes 196616 | tf_op jit(solution)/shard_map/ppermute | solution.py:188
  7.5 0.7 %collective-permute-start.2 = (bf16[128,256]{1,0:T(8,128)(2,1)S(1)}, bf16[128,256]{1,0:T(8,128)(2,1)S(1)}, u32[]{:S(2)}, u32[]{:S(2)}) collective-permute-start(bf16[128,256]{1,0:T(8,128)(2,1)S(1)} %get-tuple-element.29), channel_id=1, source_target_pairs={{0,4},{4,8},{8,12},{12,0},{1,5},{5,9},{9,13},{13,1},{2,6},{6,10},{... | collective-permute-start | bytes 196616 | tf_op jit(solution)/shard_map/ppermute | solution.py:188
  8.1 1.6 %collective-permute-start.3 = (bf16[128,256]{1,0:T(8,128)(2,1)S(1)}, bf16[128,256]{1,0:T(8,128)(2,1)S(1)}, u32[]{:S(2)}, u32[]{:S(2)}) collective-permute-start(bf16[128,256]{1,0:T(8,128)(2,1)S(1)} %get-tuple-element.31), channel_id=1, source_target_pairs={{0,4},{4,8},{8,12},{12,0},{1,5},{5,9},{9,13},{13,1},{2,6},{6,10},{... | collective-permute-start | bytes 196616 | tf_op jit(solution)/shard_map/ppermute | solution.py:188
  9.7 2.1 %collective-permute-start.4 = (bf16[128,256]{1,0:T(8,128)(2,1)S(1)}, bf16[128,256]{1,0:T(8,128)(2,1)S(1)}, u32[]{:S(2)}, u32[]{:S(2)}) collective-permute-start(bf16[128,256]{1,0:T(8,128)(2,1)S(1)} %get-tuple-element.32), channel_id=1, source_target_pairs={{0,8},{4,12},{8,0},{12,4},{1,9},{5,13},{9,1},{13,5},{2,10},{6,14},... | collective-permute-start | bytes 196616 | tf_op jit(solution)/shard_map/ppermute | solution.py:188
  11.8 0.0 collective-permute-done.anchor.refs_1_
  11.8 3.1 %collective-permute-start.5 = (bf16[128,256]{1,0:T(8,128)(2,1)S(1)}, bf16[128,256]{1,0:T(8,128)(2,1)S(1)}, u32[]{:S(2)}, u32[]{:S(2)}) collective-permute-start(bf16[128,256]{1,0:T(8,128)(2,1)S(1)} %get-tuple-element.33), channel_id=1, source_target_pairs={{0,12},{4,0},{8,4},{12,8},{1,13},{5,1},{9,5},{13,9},{2,14},{6,2},{... | collective-permute-start | bytes 196616 | tf_op jit(solution)/shard_map/ppermute | solution.py:188
  14.9 1.4 %shard_map.78 = (bf16[1024,512]{1,0:T(8,128)(2,1)S(1)}, f32[1,1024]{1,0:T(1,128)S(1)}) custom-call(bf16[1024,512]{1,0:T(8,128)(2,1)} %constant.2.clone.table, f32[1,1024]{1,0:T(1,128)S(1)} %bitcast.1, bf16[128,256]{1,0:T(8,128)(2,1)S(1)} %collective-permute-done.anchor.refs_1_), custom_call_target="tpu_custom_call" | custom-call | bytes 2170880 | tf_op jit(solution)/shard_map/pallas_call | solution.py:32
  16.3 0.0 collective-permute-done.1.refs_2_
  16.3 0.1 collective-permute-start.9
  16.4 0.0 collective-permute-done.2.refs_3_
  16.4 0.5 %collective-permute-start.10 = (bf16[128,256]{1,0:T(8,128)(2,1)S(1)}, bf16[128,256]{1,0:T(8,128)(2,1)S(1)}, u32[]{:S(2)}, u32[]{:S(2)}) collective-permute-start(bf16[128,256]{1,0:T(8,128)(2,1)S(1)} %get-tuple-element.42), channel_id=1, source_target_pairs={{0,8},{4,12},{8,0},{12,4},{1,9},{5,13},{9,1},{13,5},{2,10},{6,14},... | collective-permute-start | bytes 196616 | tf_op jit(solution)/shard_map/ppermute | solution.py:188
  16.9 0.0 collective-permute-done.3.refs_5_
  16.9 3.3 %collective-permute-start.11 = (bf16[128,256]{1,0:T(8,128)(2,1)S(1)}, bf16[128,256]{1,0:T(8,128)(2,1)S(1)}, u32[]{:S(2)}, u32[]{:S(2)}) collective-permute-start(bf16[128,256]{1,0:T(8,128)(2,1)S(1)} %get-tuple-element.43), channel_id=1, source_target_pairs={{0,12},{4,0},{8,4},{12,8},{1,13},{5,1},{9,5},{13,9},{2,14},{6,2},{... | collective-permute-start | bytes 196616 | tf_op jit(solution)/shard_map/ppermute | solution.py:188
  20.3 0.0 collective-permute-done.4.refs_6_
  20.3 1.6 %shard_map.79 = (f32[1024,256]{1,0:T(8,128)S(1)}, bf16[128,256]{1,0:T(8,128)(2,1)S(1)}, bf16[128,256]{1,0:T(8,128)(2,1)S(1)}, bf16[128,256]{1,0:T(8,128)(2,1)S(1)}, bf16[128,256]{1,0:T(8,128)(2,1)S(1)}) custom-call(f32[1,1024]{1,0:T(1,128)S(1)} %get-tuple-element.26.gain, bf16[128,256]{1,0:T(8,128)(2,1)S(1)} %get-tuple-element.27.refs_0_, ...), custom_call_target="tpu_custom_call" | custom-call | flops 805306368 | bytes 2887680 | tf_op jit(solution)/shard_map/pallas_call | solution.py:32
  21.9 0.6 %collective-permute-start.6 = (bf16[128,256]{1,0:T(8,128)(2,1)S(1)}, bf16[128,256]{1,0:T(8,128)(2,1)S(1)}, u32[]{:S(2)}, u32[]{:S(2)}) collective-permute-start(bf16[128,256]{1,0:T(8,128)(2,1)S(1)} %get-tuple-element.36), channel_id=1, source_target_pairs={{0,4},{4,8},{8,12},{12,0},{1,5},{5,9},{9,13},{13,1},{2,6},{6,10},{... | collective-permute-start | bytes 196616 | tf_op jit(solution)/shard_map/ppermute | solution.py:188
  22.5 2.4 %collective-permute-start.7 = (bf16[128,256]{1,0:T(8,128)(2,1)S(1)}, bf16[128,256]{1,0:T(8,128)(2,1)S(1)}, u32[]{:S(2)}, u32[]{:S(2)}) collective-permute-start(bf16[128,256]{1,0:T(8,128)(2,1)S(1)} %get-tuple-element.37), channel_id=1, source_target_pairs={{0,8},{4,12},{8,0},{12,4},{1,9},{5,13},{9,1},{13,5},{2,10},{6,14},... | collective-permute-start | bytes 196616 | tf_op jit(solution)/shard_map/ppermute | solution.py:188
  24.9 0.0 collective-permute-done.9.refs_1_
  24.9 1.9 %collective-permute-start.8 = (bf16[128,256]{1,0:T(8,128)(2,1)S(1)}, bf16[128,256]{1,0:T(8,128)(2,1)S(1)}, u32[]{:S(2)}, u32[]{:S(2)}) collective-permute-start(bf16[128,256]{1,0:T(8,128)(2,1)S(1)} %get-tuple-element.38), channel_id=1, source_target_pairs={{0,12},{4,0},{8,4},{12,8},{1,13},{5,1},{9,5},{13,9},{2,14},{6,2},{... | collective-permute-start | bytes 196616 | tf_op jit(solution)/shard_map/ppermute | solution.py:188
  26.9 1.3 %shard_map.81 = (bf16[128,256]{1,0:T(8,128)(2,1)S(1)}, bf16[128,256]{1,0:T(8,128)(2,1)S(1)}, bf16[128,256]{1,0:T(8,128)(2,1)S(1)}, bf16[128,256]{1,0:T(8,128)(2,1)S(1)}) custom-call(f32[1024,256]{1,0:T(8,128)S(1)} %get-tuple-element.39.spec, bf16[128,256]{1,0:T(8,128)(2,1)S(1)} %get-tuple-element.40.refs_0_, ...), custom_call_target="tpu_custom_call" | custom-call | flops 536870912 | bytes 2621440 | tf_op jit(solution)/shard_map/pallas_call | solution.py:32
  28.2 0.2 collective-permute-start.12
  28.4 1.9 %collective-permute-start.13 = (bf16[128,256]{1,0:T(8,128)(2,1)S(1)}, bf16[128,256]{1,0:T(8,128)(2,1)S(1)}, u32[]{:S(2)}, u32[]{:S(2)}) collective-permute-start(bf16[128,256]{1,0:T(8,128)(2,1)S(1)} %get-tuple-element.46), channel_id=1, source_target_pairs={{0,8},{4,12},{8,0},{12,4},{1,9},{5,13},{9,1},{13,5},{2,10},{6,14},... | collective-permute-start | bytes 196616 | tf_op jit(solution)/shard_map/ppermute | solution.py:188
  30.3 0.0 collective-permute-done.6.refs_1_
  30.3 1.8 %collective-permute-start.14 = (bf16[128,256]{1,0:T(8,128)(2,1)S(1)}, bf16[128,256]{1,0:T(8,128)(2,1)S(1)}, u32[]{:S(2)}, u32[]{:S(2)}) collective-permute-start(bf16[128,256]{1,0:T(8,128)(2,1)S(1)} %get-tuple-element.47), channel_id=1, source_target_pairs={{0,12},{4,0},{8,4},{12,8},{1,13},{5,1},{9,5},{13,9},{2,14},{6,2},{... | collective-permute-start | bytes 196616 | tf_op jit(solution)/shard_map/ppermute | solution.py:188
  32.1 0.0 collective-permute-done.7.refs_2_
  32.1 0.0 collective-permute-done.8.refs_3_
  32.1 0.7 %shard_map.80 = bf16[128,1024]{1,0:T(8,128)(2,1)} custom-call(bf16[128,256]{1,0:T(8,128)(2,1)S(1)} %get-tuple-element.35.refs_0_, bf16[128,256]{1,0:T(8,128)(2,1)S(1)} %collective-permute-done.6.refs_1_, bf16[128,256]{1,0:T(8,128)(2,1)S(1)} %collective-permute-done.7.refs_2_, bf16[128,256]{1,0:T(8,128)(2,1)S(1)} %collective-permute-done.8.refs_3_), custom_call_target="tpu_custom_call" | custom-call | bytes 524288 | tf_op jit(solution)/shard_map/pallas_call | solution.py:32
  32.9 1.6 %collective-permute-done.12.refs_1_ = bf16[128,256]{1,0:T(8,128)(2,1)S(1)} collective-permute-done((bf16[128,256]{1,0:T(8,128)(2,1)S(1)}, bf16[128,256]{1,0:T(8,128)(2,1)S(1)}, u32[]{:S(2)}, u32[]{:S(2)}) %collective-permute-start.12) | collective-permute-done | bytes 65568 | tf_op jit(solution)/shard_map/ppermute | solution.py:188
  34.4 0.7 %collective-permute-done.13.refs_2_ = bf16[128,256]{1,0:T(8,128)(2,1)S(1)} collective-permute-done((bf16[128,256]{1,0:T(8,128)(2,1)S(1)}, bf16[128,256]{1,0:T(8,128)(2,1)S(1)}, u32[]{:S(2)}, u32[]{:S(2)}) %collective-permute-start.13) | collective-permute-done | bytes 65568 | tf_op jit(solution)/shard_map/ppermute | solution.py:188
  35.1 0.8 %shard_map.82 = f32[128,1024]{1,0:T(8,128)} custom-call(bf16[128,256]{1,0:T(8,128)(2,1)S(1)} %get-tuple-element.44.refs_0_, bf16[128,256]{1,0:T(8,128)(2,1)S(1)} %collective-permute-done.12.refs_1_, bf16[128,256]{1,0:T(8,128)(2,1)S(1)} %collective-permute-done.13.refs_2_, bf16[128,256]{1,0:T(8,128)(2,1)S(1)} %collective-permute-done.14.refs_3_), custom_call_target="tpu_custom_call" | custom-call | bytes 786432 | tf_op jit(solution)/shard_map/pallas_call | solution.py:32
  (6 shorter events, 0.0 us)
Async XLA Ops:
  2.0 9.8 %collective-permute-start = (bf16[128,256]{1,0:T(8,128)(2,1)S(1)}, bf16[128,256]{1,0:T(8,128)(2,1)S(1)}, u32[]{:S(2)}, u32[]{:S(2)}) collective-permute-start(bf16[128,256]{1,0:T(8,128)(2,1)S(1)} %get-tuple-element.25), channel_id=1, source_target_pairs={{0,8},{4,12},{8,0},{12,4},{1,9},{5,13},{9,1},{13,5},{2,10},{6,14},... | collective-permute-start | bytes 196616 | tf_op jit(solution)/shard_map/ppermute | solution.py:188
  6.1 10.2 %collective-permute-start.1 = (bf16[128,256]{1,0:T(8,128)(2,1)S(1)}, bf16[128,256]{1,0:T(8,128)(2,1)S(1)}, u32[]{:S(2)}, u32[]{:S(2)}) collective-permute-start(bf16[128,256]{1,0:T(8,128)(2,1)S(1)} %get-tuple-element.28), channel_id=1, source_target_pairs={{0,12},{4,0},{8,4},{12,8},{1,13},{5,1},{9,5},{13,9},{2,14},{6,2},{... | collective-permute-start | bytes 196616 | tf_op jit(solution)/shard_map/ppermute | solution.py:188
  7.5 7.5 %copy-start = (f32[1024]{0:T(1024)S(1)}, f32[1024]{0:T(1024)}, u32[]{:S(2)}) copy-start(f32[1024]{0:T(1024)} %param.10) | copy-start | bytes 12292
  7.5 8.9 %collective-permute-start.2 = (bf16[128,256]{1,0:T(8,128)(2,1)S(1)}, bf16[128,256]{1,0:T(8,128)(2,1)S(1)}, u32[]{:S(2)}, u32[]{:S(2)}) collective-permute-start(bf16[128,256]{1,0:T(8,128)(2,1)S(1)} %get-tuple-element.29), channel_id=1, source_target_pairs={{0,4},{4,8},{8,12},{12,0},{1,5},{5,9},{9,13},{13,1},{2,6},{6,10},{... | collective-permute-start | bytes 196616 | tf_op jit(solution)/shard_map/ppermute | solution.py:188
  8.1 8.8 %collective-permute-start.3 = (bf16[128,256]{1,0:T(8,128)(2,1)S(1)}, bf16[128,256]{1,0:T(8,128)(2,1)S(1)}, u32[]{:S(2)}, u32[]{:S(2)}) collective-permute-start(bf16[128,256]{1,0:T(8,128)(2,1)S(1)} %get-tuple-element.31), channel_id=1, source_target_pairs={{0,4},{4,8},{8,12},{12,0},{1,5},{5,9},{9,13},{13,1},{2,6},{6,10},{... | collective-permute-start | bytes 196616 | tf_op jit(solution)/shard_map/ppermute | solution.py:188
  9.7 10.6 %collective-permute-start.4 = (bf16[128,256]{1,0:T(8,128)(2,1)S(1)}, bf16[128,256]{1,0:T(8,128)(2,1)S(1)}, u32[]{:S(2)}, u32[]{:S(2)}) collective-permute-start(bf16[128,256]{1,0:T(8,128)(2,1)S(1)} %get-tuple-element.32), channel_id=1, source_target_pairs={{0,8},{4,12},{8,0},{12,4},{1,9},{5,13},{9,1},{13,5},{2,10},{6,14},... | collective-permute-start | bytes 196616 | tf_op jit(solution)/shard_map/ppermute | solution.py:188
  11.8 8.4 %collective-permute-start.5 = (bf16[128,256]{1,0:T(8,128)(2,1)S(1)}, bf16[128,256]{1,0:T(8,128)(2,1)S(1)}, u32[]{:S(2)}, u32[]{:S(2)}) collective-permute-start(bf16[128,256]{1,0:T(8,128)(2,1)S(1)} %get-tuple-element.33), channel_id=1, source_target_pairs={{0,12},{4,0},{8,4},{12,8},{1,13},{5,1},{9,5},{13,9},{2,14},{6,2},{... | collective-permute-start | bytes 196616 | tf_op jit(solution)/shard_map/ppermute | solution.py:188
  16.3 8.6 %collective-permute-start.9 = (bf16[128,256]{1,0:T(8,128)(2,1)S(1)}, bf16[128,256]{1,0:T(8,128)(2,1)S(1)}, u32[]{:S(2)}, u32[]{:S(2)}) collective-permute-start(bf16[128,256]{1,0:T(8,128)(2,1)S(1)} %get-tuple-element.41), channel_id=1, source_target_pairs={{0,4},{4,8},{8,12},{12,0},{1,5},{5,9},{9,13},{13,1},{2,6},{6,10},{... | collective-permute-start | bytes 196616 | tf_op jit(solution)/shard_map/ppermute | solution.py:188
  16.4 10.5 %collective-permute-start.10 = (bf16[128,256]{1,0:T(8,128)(2,1)S(1)}, bf16[128,256]{1,0:T(8,128)(2,1)S(1)}, u32[]{:S(2)}, u32[]{:S(2)}) collective-permute-start(bf16[128,256]{1,0:T(8,128)(2,1)S(1)} %get-tuple-element.42), channel_id=1, source_target_pairs={{0,8},{4,12},{8,0},{12,4},{1,9},{5,13},{9,1},{13,5},{2,10},{6,14},... | collective-permute-start | bytes 196616 | tf_op jit(solution)/shard_map/ppermute | solution.py:188
  16.9 9.9 %collective-permute-start.11 = (bf16[128,256]{1,0:T(8,128)(2,1)S(1)}, bf16[128,256]{1,0:T(8,128)(2,1)S(1)}, u32[]{:S(2)}, u32[]{:S(2)}) collective-permute-start(bf16[128,256]{1,0:T(8,128)(2,1)S(1)} %get-tuple-element.43), channel_id=1, source_target_pairs={{0,12},{4,0},{8,4},{12,8},{1,13},{5,1},{9,5},{13,9},{2,14},{6,2},{... | collective-permute-start | bytes 196616 | tf_op jit(solution)/shard_map/ppermute | solution.py:188
  21.9 8.4 %collective-permute-start.6 = (bf16[128,256]{1,0:T(8,128)(2,1)S(1)}, bf16[128,256]{1,0:T(8,128)(2,1)S(1)}, u32[]{:S(2)}, u32[]{:S(2)}) collective-permute-start(bf16[128,256]{1,0:T(8,128)(2,1)S(1)} %get-tuple-element.36), channel_id=1, source_target_pairs={{0,4},{4,8},{8,12},{12,0},{1,5},{5,9},{9,13},{13,1},{2,6},{6,10},{... | collective-permute-start | bytes 196616 | tf_op jit(solution)/shard_map/ppermute | solution.py:188
  22.5 9.7 %collective-permute-start.7 = (bf16[128,256]{1,0:T(8,128)(2,1)S(1)}, bf16[128,256]{1,0:T(8,128)(2,1)S(1)}, u32[]{:S(2)}, u32[]{:S(2)}) collective-permute-start(bf16[128,256]{1,0:T(8,128)(2,1)S(1)} %get-tuple-element.37), channel_id=1, source_target_pairs={{0,8},{4,12},{8,0},{12,4},{1,9},{5,13},{9,1},{13,5},{2,10},{6,14},... | collective-permute-start | bytes 196616 | tf_op jit(solution)/shard_map/ppermute | solution.py:188
  24.9 7.2 %collective-permute-start.8 = (bf16[128,256]{1,0:T(8,128)(2,1)S(1)}, bf16[128,256]{1,0:T(8,128)(2,1)S(1)}, u32[]{:S(2)}, u32[]{:S(2)}) collective-permute-start(bf16[128,256]{1,0:T(8,128)(2,1)S(1)} %get-tuple-element.38), channel_id=1, source_target_pairs={{0,12},{4,0},{8,4},{12,8},{1,13},{5,1},{9,5},{13,9},{2,14},{6,2},{... | collective-permute-start | bytes 196616 | tf_op jit(solution)/shard_map/ppermute | solution.py:188
  28.2 6.2 %collective-permute-start.12 = (bf16[128,256]{1,0:T(8,128)(2,1)S(1)}, bf16[128,256]{1,0:T(8,128)(2,1)S(1)}, u32[]{:S(2)}, u32[]{:S(2)}) collective-permute-start(bf16[128,256]{1,0:T(8,128)(2,1)S(1)} %get-tuple-element.45), channel_id=1, source_target_pairs={{0,4},{4,8},{8,12},{12,0},{1,5},{5,9},{9,13},{13,1},{2,6},{6,10},{... | collective-permute-start | bytes 196616 | tf_op jit(solution)/shard_map/ppermute | solution.py:188
  28.4 6.7 %collective-permute-start.13 = (bf16[128,256]{1,0:T(8,128)(2,1)S(1)}, bf16[128,256]{1,0:T(8,128)(2,1)S(1)}, u32[]{:S(2)}, u32[]{:S(2)}) collective-permute-start(bf16[128,256]{1,0:T(8,128)(2,1)S(1)} %get-tuple-element.46), channel_id=1, source_target_pairs={{0,8},{4,12},{8,0},{12,4},{1,9},{5,13},{9,1},{13,5},{2,10},{6,14},... | collective-permute-start | bytes 196616 | tf_op jit(solution)/shard_map/ppermute | solution.py:188
  30.3 4.8 %collective-permute-start.14 = (bf16[128,256]{1,0:T(8,128)(2,1)S(1)}, bf16[128,256]{1,0:T(8,128)(2,1)S(1)}, u32[]{:S(2)}, u32[]{:S(2)}) collective-permute-start(bf16[128,256]{1,0:T(8,128)(2,1)S(1)} %get-tuple-element.47), channel_id=1, source_target_pairs={{0,12},{4,0},{8,4},{12,8},{1,13},{5,1},{9,5},{13,9},{2,14},{6,2},{... | collective-permute-start | bytes 196616 | tf_op jit(solution)/shard_map/ppermute | solution.py:188

commit v4 on v3

--- a/solution.py
+++ b/solution.py
@@ -55,19 +55,23 @@
 def split_body(parts, *refs):
     sources, pieces, (held, sems) = refs[:4], refs[4:-2], refs[-2:]
     copies = [pltpu.make_async_copy(source, held.at[n], sems.at[n]) for n, source in enumerate(sources)]
-    for copy in copies:
+    for copy in copies[::-1]:
         copy.start()
     outer, gate, inputs, taps = (held.at[n] for n in range(4))
     own = lax.axis_index("ctx")
     width = outer.shape[1] // parts
-    for copy in copies:
-        copy.wait()
+    copies[3].wait()
+    for shift in range(parts):
+        pieces[shift][...] = taps[:, part(ahead(own, shift, parts), width)]
+    copies[2].wait()
+    for shift in range(parts):
+        pieces[2 * parts + shift][...] = inputs[:, part(ahead(own, shift, parts), width)]
+    copies[0].wait()
+    copies[1].wait()
     for shift in range(parts):
         lanes = part(ahead(own, shift, parts), width)
-        pieces[shift][...] = taps[:, lanes]
         product = outer[:, lanes].astype(jnp.float32) * gate[:, lanes].astype(jnp.float32)
         pieces[parts + shift][...] = product.astype(jnp.bfloat16)
-        pieces[2 * parts + shift][...] = inputs[:, lanes]
 
 
 def load_body(table, gain, anchor, table_out, gain_out, sems):

time: 36.1 us -> 36.1 us (level)
  no operation moved by 1% of the time
where the time goes in v4:
time: 36.1 us; the launch traced here: 35.9 us
  starting transfers between devices  25.7 us (71%)
  Pallas kernels  7.19 us (20%)
  waiting for transfers between devices  2.28 us (6%)
  between operations  0.7 us (2%)
    ppermute x15, starting transfers between devices, moved(): lax.ppermute(pieces[n], 'ctx', pair)  25.7 us
    pallas_call x6, Pallas kernels, call(): pl.pallas_call(body, out_shape=outs, in_specs=[pl.BlockSpec(memory_space=...  7.19 us
    ppermute x15, waiting for transfers between devices, moved(): lax.ppermute(pieces[n], 'ctx', pair)  2.28 us
  transfers between devices with their start and end apart: 15, of which 2 were waited for; matrix products, arithmetic and copies ran while one was open for 0% of the time, Pallas kernels for 14%

profile of v4, /device:TPU:0, one launch (start us, length us, event | category | flops | bytes accessed | tf_op | source)
XLA Modules:
  0.0 35.9 jit_solution(17396802384232928679)
XLA Ops:
  0.6 1.3 %shard_map.77 = (bf16[128,256]{1,0:T(8,128)(2,1)S(1)}, bf16[128,256]{1,0:T(8,128)(2,1)S(1)}, bf16[128,256]{1,0:T(8,128)(2,1)S(1)}, bf16[128,256]{1,0:T(8,128)(2,...) custom-call(bf16[128,1024]{1,0:T(8,128)(2,1)} %refs_0_.1, ...), custom_call_target="tpu_custom_call" | custom-call | flops 131072 | bytes 1835008 | tf_op jit(solution)/shard_map/pallas_call | solution.py:32
  1.9 4.1 %collective-permute-start = (bf16[128,256]{1,0:T(8,128)(2,1)S(1)}, bf16[128,256]{1,0:T(8,128)(2,1)S(1)}, u32[]{:S(2)}, u32[]{:S(2)}) collective-permute-start(bf16[128,256]{1,0:T(8,128)(2,1)S(1)} %get-tuple-element.25), channel_id=1, source_target_pairs={{0,8},{4,12},{8,0},{12,4},{1,9},{5,13},{9,1},{13,5},{2,10},{6,14},... | collective-permute-start | bytes 196616 | tf_op jit(solution)/shard_map/ppermute | solution.py:192
  6.0 1.3 %collective-permute-start.1 = (bf16[128,256]{1,0:T(8,128)(2,1)S(1)}, bf16[128,256]{1,0:T(8,128)(2,1)S(1)}, u32[]{:S(2)}, u32[]{:S(2)}) collective-permute-start(bf16[128,256]{1,0:T(8,128)(2,1)S(1)} %get-tuple-element.28), channel_id=1, source_target_pairs={{0,12},{4,0},{8,4},{12,8},{1,13},{5,1},{9,5},{13,9},{2,14},{6,2},{... | collective-permute-start | bytes 196616 | tf_op jit(solution)/shard_map/ppermute | solution.py:192
  7.4 0.7 %collective-permute-start.2 = (bf16[128,256]{1,0:T(8,128)(2,1)S(1)}, bf16[128,256]{1,0:T(8,128)(2,1)S(1)}, u32[]{:S(2)}, u32[]{:S(2)}) collective-permute-start(bf16[128,256]{1,0:T(8,128)(2,1)S(1)} %get-tuple-element.29), channel_id=1, source_target_pairs={{0,4},{4,8},{8,12},{12,0},{1,5},{5,9},{9,13},{13,1},{2,6},{6,10},{... | collective-permute-start | bytes 196616 | tf_op jit(solution)/shard_map/ppermute | solution.py:192
  8.1 1.6 %collective-permute-start.3 = (bf16[128,256]{1,0:T(8,128)(2,1)S(1)}, bf16[128,256]{1,0:T(8,128)(2,1)S(1)}, u32[]{:S(2)}, u32[]{:S(2)}) collective-permute-start(bf16[128,256]{1,0:T(8,128)(2,1)S(1)} %get-tuple-element.31), channel_id=1, source_target_pairs={{0,4},{4,8},{8,12},{12,0},{1,5},{5,9},{9,13},{13,1},{2,6},{6,10},{... | collective-permute-start | bytes 196616 | tf_op jit(solution)/shard_map/ppermute | solution.py:192
  9.6 2.1 %collective-permute-start.4 = (bf16[128,256]{1,0:T(8,128)(2,1)S(1)}, bf16[128,256]{1,0:T(8,128)(2,1)S(1)}, u32[]{:S(2)}, u32[]{:S(2)}) collective-permute-start(bf16[128,256]{1,0:T(8,128)(2,1)S(1)} %get-tuple-element.32), channel_id=1, source_target_pairs={{0,8},{4,12},{8,0},{12,4},{1,9},{5,13},{9,1},{13,5},{2,10},{6,14},... | collective-permute-start | bytes 196616 | tf_op jit(solution)/shard_map/ppermute | solution.py:192
  11.8 0.0 collective-permute-done.anchor.refs_1_
  11.8 3.1 %collective-permute-start.5 = (bf16[128,256]{1,0:T(8,128)(2,1)S(1)}, bf16[128,256]{1,0:T(8,128)(2,1)S(1)}, u32[]{:S(2)}, u32[]{:S(2)}) collective-permute-start(bf16[128,256]{1,0:T(8,128)(2,1)S(1)} %get-tuple-element.33), channel_id=1, source_target_pairs={{0,12},{4,0},{8,4},{12,8},{1,13},{5,1},{9,5},{13,9},{2,14},{6,2},{... | collective-permute-start | bytes 196616 | tf_op jit(solution)/shard_map/ppermute | solution.py:192
  14.9 1.4 %shard_map.78 = (bf16[1024,512]{1,0:T(8,128)(2,1)S(1)}, f32[1,1024]{1,0:T(1,128)S(1)}) custom-call(bf16[1024,512]{1,0:T(8,128)(2,1)} %constant.2.clone.table, f32[1,1024]{1,0:T(1,128)S(1)} %bitcast.1, bf16[128,256]{1,0:T(8,128)(2,1)S(1)} %collective-permute-done.anchor.refs_1_), custom_call_target="tpu_custom_call" | custom-call | bytes 2170880 | tf_op jit(solution)/shard_map/pallas_call | solution.py:32
  16.2 0.1 collective-permute-start.9
  16.3 0.5 %collective-permute-start.10 = (bf16[128,256]{1,0:T(8,128)(2,1)S(1)}, bf16[128,256]{1,0:T(8,128)(2,1)S(1)}, u32[]{:S(2)}, u32[]{:S(2)}) collective-permute-start(bf16[128,256]{1,0:T(8,128)(2,1)S(1)} %get-tuple-element.42), channel_id=1, source_target_pairs={{0,8},{4,12},{8,0},{12,4},{1,9},{5,13},{9,1},{13,5},{2,10},{6,14},... | collective-permute-start | bytes 196616 | tf_op jit(solution)/shard_map/ppermute | solution.py:192
  16.9 3.3 %collective-permute-start.11 = (bf16[128,256]{1,0:T(8,128)(2,1)S(1)}, bf16[128,256]{1,0:T(8,128)(2,1)S(1)}, u32[]{:S(2)}, u32[]{:S(2)}) collective-permute-start(bf16[128,256]{1,0:T(8,128)(2,1)S(1)} %get-tuple-element.43), channel_id=1, source_target_pairs={{0,12},{4,0},{8,4},{12,8},{1,13},{5,1},{9,5},{13,9},{2,14},{6,2},{... | collective-permute-start | bytes 196616 | tf_op jit(solution)/shard_map/ppermute | solution.py:192
  20.2 0.0 collective-permute-done.4.refs_6_
  20.2 0.0 collective-permute-done.5.refs_7_
  20.2 1.6 %shard_map.79 = (f32[1024,256]{1,0:T(8,128)S(1)}, bf16[128,256]{1,0:T(8,128)(2,1)S(1)}, bf16[128,256]{1,0:T(8,128)(2,1)S(1)}, bf16[128,256]{1,0:T(8,128)(2,1)S(1)}, bf16[128,256]{1,0:T(8,128)(2,1)S(1)}) custom-call(f32[1,1024]{1,0:T(1,128)S(1)} %get-tuple-element.26.gain, bf16[128,256]{1,0:T(8,128)(2,1)S(1)} %get-tuple-element.27.refs_0_, ...), custom_call_target="tpu_custom_call" | custom-call | flops 805306368 | bytes 2887680 | tf_op jit(solution)/shard_map/pallas_call | solution.py:32
  21.8 0.6 %collective-permute-start.6 = (bf16[128,256]{1,0:T(8,128)(2,1)S(1)}, bf16[128,256]{1,0:T(8,128)(2,1)S(1)}, u32[]{:S(2)}, u32[]{:S(2)}) collective-permute-start(bf16[128,256]{1,0:T(8,128)(2,1)S(1)} %get-tuple-element.36), channel_id=1, source_target_pairs={{0,4},{4,8},{8,12},{12,0},{1,5},{5,9},{9,13},{13,1},{2,6},{6,10},{... | collective-permute-start | bytes 196616 | tf_op jit(solution)/shard_map/ppermute | solution.py:192
  22.4 2.4 %collective-permute-start.7 = (bf16[128,256]{1,0:T(8,128)(2,1)S(1)}, bf16[128,256]{1,0:T(8,128)(2,1)S(1)}, u32[]{:S(2)}, u32[]{:S(2)}) collective-permute-start(bf16[128,256]{1,0:T(8,128)(2,1)S(1)} %get-tuple-element.37), channel_id=1, source_target_pairs={{0,8},{4,12},{8,0},{12,4},{1,9},{5,13},{9,1},{13,5},{2,10},{6,14},... | collective-permute-start | bytes 196616 | tf_op jit(solution)/shard_map/ppermute | solution.py:192
  24.9 1.9 %collective-permute-start.8 = (bf16[128,256]{1,0:T(8,128)(2,1)S(1)}, bf16[128,256]{1,0:T(8,128)(2,1)S(1)}, u32[]{:S(2)}, u32[]{:S(2)}) collective-permute-start(bf16[128,256]{1,0:T(8,128)(2,1)S(1)} %get-tuple-element.38), channel_id=1, source_target_pairs={{0,12},{4,0},{8,4},{12,8},{1,13},{5,1},{9,5},{13,9},{2,14},{6,2},{... | collective-permute-start | bytes 196616 | tf_op jit(solution)/shard_map/ppermute | solution.py:192
  26.8 0.0 collective-permute-done.10.refs_2_
  26.8 0.0 collective-permute-done.11.refs_3_
  26.8 1.3 %shard_map.81 = (bf16[128,256]{1,0:T(8,128)(2,1)S(1)}, bf16[128,256]{1,0:T(8,128)(2,1)S(1)}, bf16[128,256]{1,0:T(8,128)(2,1)S(1)}, bf16[128,256]{1,0:T(8,128)(2,1)S(1)}) custom-call(f32[1024,256]{1,0:T(8,128)S(1)} %get-tuple-element.39.spec, bf16[128,256]{1,0:T(8,128)(2,1)S(1)} %get-tuple-element.40.refs_0_, ...), custom_call_target="tpu_custom_call" | custom-call | flops 536870912 | bytes 2621440 | tf_op jit(solution)/shard_map/pallas_call | solution.py:32
  28.1 0.2 collective-permute-start.12
  28.4 1.8 %collective-permute-start.13 = (bf16[128,256]{1,0:T(8,128)(2,1)S(1)}, bf16[128,256]{1,0:T(8,128)(2,1)S(1)}, u32[]{:S(2)}, u32[]{:S(2)}) collective-permute-start(bf16[128,256]{1,0:T(8,128)(2,1)S(1)} %get-tuple-element.46), channel_id=1, source_target_pairs={{0,8},{4,12},{8,0},{12,4},{1,9},{5,13},{9,1},{13,5},{2,10},{6,14},... | collective-permute-start | bytes 196616 | tf_op jit(solution)/shard_map/ppermute | solution.py:192
  30.2 0.0 collective-permute-done.6.refs_1_
  30.2 1.9 %collective-permute-start.14 = (bf16[128,256]{1,0:T(8,128)(2,1)S(1)}, bf16[128,256]{1,0:T(8,128)(2,1)S(1)}, u32[]{:S(2)}, u32[]{:S(2)}) collective-permute-start(bf16[128,256]{1,0:T(8,128)(2,1)S(1)} %get-tuple-element.47), channel_id=1, source_target_pairs={{0,12},{4,0},{8,4},{12,8},{1,13},{5,1},{9,5},{13,9},{2,14},{6,2},{... | collective-permute-start | bytes 196616 | tf_op jit(solution)/shard_map/ppermute | solution.py:192
  32.1 0.0 collective-permute-done.7.refs_2_
  32.1 0.0 collective-permute-done.8.refs_3_
  32.1 0.7 %shard_map.80 = bf16[128,1024]{1,0:T(8,128)(2,1)} custom-call(bf16[128,256]{1,0:T(8,128)(2,1)S(1)} %get-tuple-element.35.refs_0_, bf16[128,256]{1,0:T(8,128)(2,1)S(1)} %collective-permute-done.6.refs_1_, bf16[128,256]{1,0:T(8,128)(2,1)S(1)} %collective-permute-done.7.refs_2_, bf16[128,256]{1,0:T(8,128)(2,1)S(1)} %collective-permute-done.8.refs_3_), custom_call_target="tpu_custom_call" | custom-call | bytes 524288 | tf_op jit(solution)/shard_map/pallas_call | solution.py:32
  32.8 1.6 %collective-permute-done.12.refs_1_ = bf16[128,256]{1,0:T(8,128)(2,1)S(1)} collective-permute-done((bf16[128,256]{1,0:T(8,128)(2,1)S(1)}, bf16[128,256]{1,0:T(8,128)(2,1)S(1)}, u32[]{:S(2)}, u32[]{:S(2)}) %collective-permute-start.12) | collective-permute-done | bytes 65568 | tf_op jit(solution)/shard_map/ppermute | solution.py:192
  34.4 0.7 %collective-permute-done.13.refs_2_ = bf16[128,256]{1,0:T(8,128)(2,1)S(1)} collective-permute-done((bf16[128,256]{1,0:T(8,128)(2,1)S(1)}, bf16[128,256]{1,0:T(8,128)(2,1)S(1)}, u32[]{:S(2)}, u32[]{:S(2)}) %collective-permute-start.13) | collective-permute-done | bytes 65568 | tf_op jit(solution)/shard_map/ppermute | solution.py:192
  35.1 0.0 collective-permute-done.14.refs_3_
  35.1 0.8 %shard_map.82 = f32[128,1024]{1,0:T(8,128)} custom-call(bf16[128,256]{1,0:T(8,128)(2,1)S(1)} %get-tuple-element.44.refs_0_, bf16[128,256]{1,0:T(8,128)(2,1)S(1)} %collective-permute-done.12.refs_1_, bf16[128,256]{1,0:T(8,128)(2,1)S(1)} %collective-permute-done.13.refs_2_, bf16[128,256]{1,0:T(8,128)(2,1)S(1)} %collective-permute-done.14.refs_3_), custom_call_target="tpu_custom_call" | custom-call | bytes 786432 | tf_op jit(solution)/shard_map/pallas_call | solution.py:32
  (6 shorter events, 0.0 us)
Async XLA Ops:
  1.9 9.8 %collective-permute-start = (bf16[128,256]{1,0:T(8,128)(2,1)S(1)}, bf16[128,256]{1,0:T(8,128)(2,1)S(1)}, u32[]{:S(2)}, u32[]{:S(2)}) collective-permute-start(bf16[128,256]{1,0:T(8,128)(2,1)S(1)} %get-tuple-element.25), channel_id=1, source_target_pairs={{0,8},{4,12},{8,0},{12,4},{1,9},{5,13},{9,1},{13,5},{2,10},{6,14},... | collective-permute-start | bytes 196616 | tf_op jit(solution)/shard_map/ppermute | solution.py:192
  6.0 10.2 %collective-permute-start.1 = (bf16[128,256]{1,0:T(8,128)(2,1)S(1)}, bf16[128,256]{1,0:T(8,128)(2,1)S(1)}, u32[]{:S(2)}, u32[]{:S(2)}) collective-permute-start(bf16[128,256]{1,0:T(8,128)(2,1)S(1)} %get-tuple-element.28), channel_id=1, source_target_pairs={{0,12},{4,0},{8,4},{12,8},{1,13},{5,1},{9,5},{13,9},{2,14},{6,2},{... | collective-permute-start | bytes 196616 | tf_op jit(solution)/shard_map/ppermute | solution.py:192
  7.4 7.5 %copy-start = (f32[1024]{0:T(1024)S(1)}, f32[1024]{0:T(1024)}, u32[]{:S(2)}) copy-start(f32[1024]{0:T(1024)} %param.10) | copy-start | bytes 12292
  7.4 8.9 %collective-permute-start.2 = (bf16[128,256]{1,0:T(8,128)(2,1)S(1)}, bf16[128,256]{1,0:T(8,128)(2,1)S(1)}, u32[]{:S(2)}, u32[]{:S(2)}) collective-permute-start(bf16[128,256]{1,0:T(8,128)(2,1)S(1)} %get-tuple-element.29), channel_id=1, source_target_pairs={{0,4},{4,8},{8,12},{12,0},{1,5},{5,9},{9,13},{13,1},{2,6},{6,10},{... | collective-permute-start | bytes 196616 | tf_op jit(solution)/shard_map/ppermute | solution.py:192
  8.1 8.8 %collective-permute-start.3 = (bf16[128,256]{1,0:T(8,128)(2,1)S(1)}, bf16[128,256]{1,0:T(8,128)(2,1)S(1)}, u32[]{:S(2)}, u32[]{:S(2)}) collective-permute-start(bf16[128,256]{1,0:T(8,128)(2,1)S(1)} %get-tuple-element.31), channel_id=1, source_target_pairs={{0,4},{4,8},{8,12},{12,0},{1,5},{5,9},{9,13},{13,1},{2,6},{6,10},{... | collective-permute-start | bytes 196616 | tf_op jit(solution)/shard_map/ppermute | solution.py:192
  9.6 10.6 %collective-permute-start.4 = (bf16[128,256]{1,0:T(8,128)(2,1)S(1)}, bf16[128,256]{1,0:T(8,128)(2,1)S(1)}, u32[]{:S(2)}, u32[]{:S(2)}) collective-permute-start(bf16[128,256]{1,0:T(8,128)(2,1)S(1)} %get-tuple-element.32), channel_id=1, source_target_pairs={{0,8},{4,12},{8,0},{12,4},{1,9},{5,13},{9,1},{13,5},{2,10},{6,14},... | collective-permute-start | bytes 196616 | tf_op jit(solution)/shard_map/ppermute | solution.py:192
  11.8 8.4 %collective-permute-start.5 = (bf16[128,256]{1,0:T(8,128)(2,1)S(1)}, bf16[128,256]{1,0:T(8,128)(2,1)S(1)}, u32[]{:S(2)}, u32[]{:S(2)}) collective-permute-start(bf16[128,256]{1,0:T(8,128)(2,1)S(1)} %get-tuple-element.33), channel_id=1, source_target_pairs={{0,12},{4,0},{8,4},{12,8},{1,13},{5,1},{9,5},{13,9},{2,14},{6,2},{... | collective-permute-start | bytes 196616 | tf_op jit(solution)/shard_map/ppermute | solution.py:192
  16.2 8.6 %collective-permute-start.9 = (bf16[128,256]{1,0:T(8,128)(2,1)S(1)}, bf16[128,256]{1,0:T(8,128)(2,1)S(1)}, u32[]{:S(2)}, u32[]{:S(2)}) collective-permute-start(bf16[128,256]{1,0:T(8,128)(2,1)S(1)} %get-tuple-element.41), channel_id=1, source_target_pairs={{0,4},{4,8},{8,12},{12,0},{1,5},{5,9},{9,13},{13,1},{2,6},{6,10},{... | collective-permute-start | bytes 196616 | tf_op jit(solution)/shard_map/ppermute | solution.py:192
  16.3 10.5 %collective-permute-start.10 = (bf16[128,256]{1,0:T(8,128)(2,1)S(1)}, bf16[128,256]{1,0:T(8,128)(2,1)S(1)}, u32[]{:S(2)}, u32[]{:S(2)}) collective-permute-start(bf16[128,256]{1,0:T(8,128)(2,1)S(1)} %get-tuple-element.42), channel_id=1, source_target_pairs={{0,8},{4,12},{8,0},{12,4},{1,9},{5,13},{9,1},{13,5},{2,10},{6,14},... | collective-permute-start | bytes 196616 | tf_op jit(solution)/shard_map/ppermute | solution.py:192
  16.9 9.9 %collective-permute-start.11 = (bf16[128,256]{1,0:T(8,128)(2,1)S(1)}, bf16[128,256]{1,0:T(8,128)(2,1)S(1)}, u32[]{:S(2)}, u32[]{:S(2)}) collective-permute-start(bf16[128,256]{1,0:T(8,128)(2,1)S(1)} %get-tuple-element.43), channel_id=1, source_target_pairs={{0,12},{4,0},{8,4},{12,8},{1,13},{5,1},{9,5},{13,9},{2,14},{6,2},{... | collective-permute-start | bytes 196616 | tf_op jit(solution)/shard_map/ppermute | solution.py:192
  21.8 8.4 %collective-permute-start.6 = (bf16[128,256]{1,0:T(8,128)(2,1)S(1)}, bf16[128,256]{1,0:T(8,128)(2,1)S(1)}, u32[]{:S(2)}, u32[]{:S(2)}) collective-permute-start(bf16[128,256]{1,0:T(8,128)(2,1)S(1)} %get-tuple-element.36), channel_id=1, source_target_pairs={{0,4},{4,8},{8,12},{12,0},{1,5},{5,9},{9,13},{13,1},{2,6},{6,10},{... | collective-permute-start | bytes 196616 | tf_op jit(solution)/shard_map/ppermute | solution.py:192
  22.4 9.7 %collective-permute-start.7 = (bf16[128,256]{1,0:T(8,128)(2,1)S(1)}, bf16[128,256]{1,0:T(8,128)(2,1)S(1)}, u32[]{:S(2)}, u32[]{:S(2)}) collective-permute-start(bf16[128,256]{1,0:T(8,128)(2,1)S(1)} %get-tuple-element.37), channel_id=1, source_target_pairs={{0,8},{4,12},{8,0},{12,4},{1,9},{5,13},{9,1},{13,5},{2,10},{6,14},... | collective-permute-start | bytes 196616 | tf_op jit(solution)/shard_map/ppermute | solution.py:192
  24.9 7.2 %collective-permute-start.8 = (bf16[128,256]{1,0:T(8,128)(2,1)S(1)}, bf16[128,256]{1,0:T(8,128)(2,1)S(1)}, u32[]{:S(2)}, u32[]{:S(2)}) collective-permute-start(bf16[128,256]{1,0:T(8,128)(2,1)S(1)} %get-tuple-element.38), channel_id=1, source_target_pairs={{0,12},{4,0},{8,4},{12,8},{1,13},{5,1},{9,5},{13,9},{2,14},{6,2},{... | collective-permute-start | bytes 196616 | tf_op jit(solution)/shard_map/ppermute | solution.py:192
  28.1 6.2 %collective-permute-start.12 = (bf16[128,256]{1,0:T(8,128)(2,1)S(1)}, bf16[128,256]{1,0:T(8,128)(2,1)S(1)}, u32[]{:S(2)}, u32[]{:S(2)}) collective-permute-start(bf16[128,256]{1,0:T(8,128)(2,1)S(1)} %get-tuple-element.45), channel_id=1, source_target_pairs={{0,4},{4,8},{8,12},{12,0},{1,5},{5,9},{9,13},{13,1},{2,6},{6,10},{... | collective-permute-start | bytes 196616 | tf_op jit(solution)/shard_map/ppermute | solution.py:192
  28.4 6.7 %collective-permute-start.13 = (bf16[128,256]{1,0:T(8,128)(2,1)S(1)}, bf16[128,256]{1,0:T(8,128)(2,1)S(1)}, u32[]{:S(2)}, u32[]{:S(2)}) collective-permute-start(bf16[128,256]{1,0:T(8,128)(2,1)S(1)} %get-tuple-element.46), channel_id=1, source_target_pairs={{0,8},{4,12},{8,0},{12,4},{1,9},{5,13},{9,1},{13,5},{2,10},{6,14},... | collective-permute-start | bytes 196616 | tf_op jit(solution)/shard_map/ppermute | solution.py:192
  30.2 4.8 %collective-permute-start.14 = (bf16[128,256]{1,0:T(8,128)(2,1)S(1)}, bf16[128,256]{1,0:T(8,128)(2,1)S(1)}, u32[]{:S(2)}, u32[]{:S(2)}) collective-permute-start(bf16[128,256]{1,0:T(8,128)(2,1)S(1)} %get-tuple-element.47), channel_id=1, source_target_pairs={{0,12},{4,0},{8,4},{12,8},{1,13},{5,1},{9,5},{13,9},{2,14},{6,2},{... | collective-permute-start | bytes 196616 | tf_op jit(solution)/shard_map/ppermute | solution.py:192
